TPU v7x, 256 devices: a whole 4x4x8 slice. The times are simulated.
256 devices in a mesh: slab: 8 (over x, core), coil: 32 (over y, z).
Axes of the slice: x: 4, y: 4, z: 8, core: 2. Of those that a mesh axis runs over, the one named last changes fastest.
Arguments:
- prior_image: float32 [256, 128, 128], P(('slab', 'coil')), may hold values from -12 to 12
- coil_maps: bfloat16 [32, 256, 128, 128], P('coil', 'slab'), may hold values from -3 to 3
- kspace: bfloat16 [32, 128, 256, 128], P('coil', 'slab'), may hold values from -6 to 6
- sampling: int32 [128, 256], P('slab'), may hold values 0 or 1
- weight_first: bfloat16 [3, 3, 3, 32, 2], replicated, may hold values from -0.875 to 0.875
- bias_first: float32 [32], replicated, may hold values from -3 to 3
- weight_middle: bfloat16 [3, 3, 3, 32, 32], replicated, may hold values from -0.21875 to 0.21875
- bias_middle: float32 [32], replicated, may hold values from -3 to 3
- weight_last: bfloat16 [3, 3, 3, 2, 32], replicated, may hold values from -0.21875 to 0.21875
- bias_last: float32 [2], replicated, may hold values from -3 to 3
Outputs:
- solution: float32 [256, 128, 128], P(('slab', 'coil'))
- residual: float32 [256, 128, 128], P(('slab', 'coil'))
All inputs are finite; a program needn't handle non-finite values. No bound on the sum of `sampling` on one device may be relied on, other than what follows from the above.
Results may differ from a plain program's by a relative error of at most 0.0018.
Values may be sent and summed in bfloat16 or wider, within the bound.
A program may use at most 128 MiB of HBM per device.

v0:
```python
import math

import jax
import jax.numpy as jnp
from jax import lax
from jax.sharding import Mesh
from jax.sharding import PartitionSpec as P

CG_ITERS = 2
SLAB = ("slab_0", "slab_1")
SLAB_COIL = ("slab_0", "slab_1", "coil_0", "coil_1")
COIL = ("coil_0", "coil_1")


penalty = 0.5
highest = lax.Precision.HIGHEST


def one_axis_at_a_time(value, axes):
    for axis in axes:
        value = lax.psum(value, axis)
    return value


def with_halo(value, sides, width):
    edges = {}
    for axis, dim in sides:
        count, length = (lax.axis_size(axis), value.shape[dim])
        up = [(i, (i + 1) % count) for i in range(count - 1)]
        last = lax.slice_in_dim(value, length - width, length, axis=dim)
        initial = lax.slice_in_dim(value, 0, width, axis=dim)
        edges[dim] = (
            lax.ppermute(last, axis, up),
            lax.ppermute(initial, axis, [(b, a) for a, b in up]),
        )
    done = []
    for _, dim in sides:
        low, high = edges[dim]
        around = [(width, width) if d in done else (0, 0) for d in range(value.ndim)]
        value = jnp.concatenate([jnp.pad(low, around), value, jnp.pad(high, around)], axis=dim)
        done.append(dim)
    return value


def cut_along(value, dim, count):
    before, after = (value.shape[:dim], value.shape[dim + 1 :])
    return jnp.moveaxis(value.reshape(*before, count, -1, *after), dim, 0)


def summed_on_arrival(value, axis, dim):
    tiles = cut_along(value, dim, lax.axis_size(axis))
    arrived = lax.all_to_all(tiles, axis, split_axis=0, concat_axis=0, tiled=True)
    return arrived.sum(axis=0)


def laid_out(tiles, dim):
    tiles = jnp.moveaxis(tiles, 0, dim)
    shape = tiles.shape
    return tiles.reshape(*shape[:dim], shape[dim] * shape[dim + 1], *shape[dim + 2 :])


def sent_to_all(value, axis):
    copies = jnp.broadcast_to(value, (lax.axis_size(axis), *value.shape))
    return lax.all_to_all(copies, axis, split_axis=0, concat_axis=0, tiled=True)


def gather_directly(value, axis, dim):
    return laid_out(sent_to_all(value, axis), dim)


def dft_table(length):
    positions = jnp.arange(length, dtype=jnp.int32)
    phases = positions[:, None] * positions[None, :] % length
    angles = phases.astype(jnp.float32) * (2.0 * math.pi / length)
    return jnp.concatenate([jnp.cos(angles), jnp.sin(angles)], axis=0) / math.sqrt(length)


def combine(stacked, along_axis, inverse):
    length = stacked.shape[along_axis] // 2
    cos_part = lax.slice_in_dim(stacked, 0, length, axis=along_axis)
    sin_part = lax.slice_in_dim(stacked, length, 2 * length, axis=along_axis)
    half_width = stacked.shape[-1] // 2
    if inverse:
        real_part = cos_part[..., :half_width] - sin_part[..., half_width:]
        imag_part = cos_part[..., half_width:] + sin_part[..., :half_width]
    else:
        real_part = cos_part[..., :half_width] + sin_part[..., half_width:]
        imag_part = cos_part[..., half_width:] - sin_part[..., :half_width]
    return jnp.concatenate([real_part, imag_part], axis=-1)


def complex_product(coil_map, volume, conjugate):
    half_width = volume.shape[-1] // 2
    map_real = coil_map[..., :half_width].astype(jnp.float32)
    map_imag = coil_map[..., half_width:].astype(jnp.float32)
    if conjugate:
        map_imag = -map_imag
    field_real = volume[..., :half_width]
    field_imag = volume[..., half_width:]
    return jnp.concatenate(
        [
            map_real * field_real - map_imag * field_imag,
            map_real * field_imag + map_imag * field_real,
        ],
        axis=-1,
    )


def forward_planes(transform, volume):
    stacked = jnp.einsum(
        "kz,yzn->ykn", transform, volume, precision=highest, preferred_element_type=jnp.float32
    )
    return combine(stacked, 1, False)


def inverse_planes(transform, spectrum):
    stacked = jnp.einsum(
        "jk,kyn->yjn", transform, spectrum, precision=highest, preferred_element_type=jnp.float32
    )
    return combine(stacked, 1, True)


def transpose_slab(volume):
    return lax.all_to_all(volume, SLAB, split_axis=1, concat_axis=0, tiled=True)


def from_kspace(spectrum, y_table):
    stacked = jnp.einsum(
        "jk,zkn->zjn", y_table, spectrum, precision=highest, preferred_element_type=jnp.float32
    )
    return transpose_slab(combine(stacked, 1, True))


def through_kspace(spectrum_rows, y_table, sampled):
    moved = transpose_slab(spectrum_rows)
    stacked = jnp.einsum(
        "ky,yzn->zkn", y_table, moved, precision=highest, preferred_element_type=jnp.float32
    )
    spectrum = combine(stacked, 1, False) * sampled
    return from_kspace(spectrum, y_table)


def paired_total(first_value, second_value):
    return (one_axis_at_a_time(first_value, SLAB_COIL), one_axis_at_a_time(second_value, SLAB_COIL))


def convolve_layer(features, weights, offsets, readout):
    row_total = features.shape[0]
    in_channels = features.shape[1]
    span_cells = features.shape[2]
    out_channels = weights.shape[3]
    extended = with_halo(features, ((SLAB_COIL, 0),), 1)
    padded = jnp.pad(extended, ((0, 0), (0, 0), (readout + 1, readout + 1)))
    column = (jnp.arange(padded.shape[2], dtype=jnp.int32) - 1) % readout
    zero_value = jnp.zeros((), padded.dtype)
    sources = (
        jnp.where(column != readout - 1, padded, zero_value),
        padded,
        jnp.where(column != 0, padded, zero_value),
    )
    running = jnp.zeros((row_total, out_channels, span_cells), jnp.float32)
    for row_shift in range(3):
        for plane_shift in range(3):
            pieces = []
            for column_shift in range(3):
                first_cell = plane_shift * readout + column_shift
                pieces.append(
                    lax.slice(
                        sources[column_shift],
                        (row_shift, 0, first_cell),
                        (row_shift + row_total, in_channels, first_cell + span_cells),
                    )
                )
            stacked = jnp.concatenate(pieces, axis=1)
            kernel = jnp.transpose(weights[row_shift, plane_shift], (1, 0, 2)).reshape(
                out_channels, 3 * in_channels
            )
            running = running + jnp.einsum(
                "oc,ycn->yon", kernel, stacked, preferred_element_type=jnp.float32
            )
    return running + offsets[None, :, None]


def body(
    prior_image,
    coil_maps,
    kspace,
    sampling,
    weight_first,
    bias_first,
    weight_middle,
    bias_middle,
    weight_last,
    bias_last,
):
    readout = prior_image.shape[2] // 2
    own_rows = prior_image.shape[0]
    planes = prior_image.shape[1]
    features = (
        jnp.stack([prior_image[..., :readout], prior_image[..., readout:]], axis=1)
        .reshape(own_rows, 2, planes * readout)
        .astype(jnp.bfloat16)
    )
    hidden = jax.nn.relu(convolve_layer(features, weight_first, bias_first, readout)).astype(
        jnp.bfloat16
    )
    hidden = jax.nn.relu(convolve_layer(hidden, weight_middle, bias_middle, readout)).astype(
        jnp.bfloat16
    )
    output = convolve_layer(hidden, weight_last, bias_last, readout).reshape(
        own_rows, 2, planes, readout
    )
    denoised = prior_image + jnp.concatenate([output[:, 0], output[:, 1]], axis=-1)
    z_table = dft_table(planes)
    y_table = dft_table(sampling.shape[1])
    sampled = sampling.astype(jnp.float32)[:, :, None]
    slab_maps = coil_maps[0]
    measured = kspace[0].astype(jnp.float32) * sampled
    data_side = from_kspace(measured, y_table)

    def reduce_coils(image_side):
        return summed_on_arrival(
            complex_product(slab_maps, inverse_planes(z_table, image_side), True), COIL, 0
        )

    def apply_operator(direction):
        spectrum = forward_planes(
            z_table, complex_product(slab_maps, gather_directly(direction, COIL, 0), False)
        )
        return reduce_coils(through_kspace(spectrum, y_table, sampled)) + penalty * direction

    right_side = reduce_coils(data_side) + penalty * denoised

    def own_inner(left_side, other_side):
        return jnp.sum(left_side * other_side)

    solution = jnp.zeros_like(right_side)
    residual = right_side
    image_res = apply_operator(residual)
    norm_now, product = paired_total(own_inner(residual, residual), own_inner(residual, image_res))
    step_size = norm_now / product
    direction = residual
    image_dir = image_res
    for iteration in range(CG_ITERS):
        solution = solution + step_size * direction
        residual = residual - step_size * image_dir
        if iteration + 1 < CG_ITERS:
            image_res = apply_operator(residual)
            norm_next, product = paired_total(
                own_inner(residual, residual), own_inner(residual, image_res)
            )
            growth = norm_next / norm_now
            step_size = norm_next / (product - growth * norm_next / step_size)
            direction = residual + growth * direction
            image_dir = image_res + growth * image_dir
            norm_now = norm_next
    return (solution, residual)


def solution(mesh):
    torus = Mesh(mesh.devices.reshape(4, 2, 4, 8), ("slab_0", "slab_1", "coil_0", "coil_1"))
    in_specs = (
        P(SLAB_COIL, None, None),
        P(COIL, SLAB, None, None),
        P(COIL, SLAB, None, None),
        P(SLAB, None),
        P(),
        P(),
        P(),
        P(),
        P(),
        P(),
    )
    out_specs = (P(SLAB_COIL, None, None), P(SLAB_COIL, None, None))
    return jax.shard_map(body, mesh=torus, in_specs=in_specs, out_specs=out_specs, check_vma=False)
```

profile of v0, /device:TPU:1, one launch (start us, length us, event | category | flops | bytes accessed | tf_op | source)
XLA Modules:
  0.0 650.6 jit_solution(10659299899708978140)
XLA Ops:
  1.8 4.4 collective-permute-start
  6.2 8.9 %collective-permute-start.1 = (bf16[1,2,8192]{2,1,0:T(2,128)(2,1)S(1)}, bf16[1,2,8192]{2,1,0:T(2,128)(2,1)S(1)}, u32[]{:S(2)}, u32[]{:S(2)}) collective-permute-start(bf16[1,2,8192]{2,1,0:T(2,128)(2,1)S(1)} %pad_maximum_fusion.5), channel_id=1, source_target_pairs={{1,0},{2,1},{3,2},{4,3},{5,4},{6,5},{7,6},{8,7},{9,8},{10,9},{11,1... | collective-permute-start | bytes 98312 | tf_op jit(solution)/shard_map/ppermute | solution.py:34
  22.6 7.7 %collective-permute-start.3 = (bf16[1,32,8192]{2,1,0:T(8,128)(2,1)S(1)}, bf16[1,32,8192]{2,1,0:T(8,128)(2,1)}, u32[]{:S(2)}, u32[]{:S(2)}) collective-permute-start(bf16[1,32,8192]{2,1,0:T(8,128)(2,1)S(1)} %fusion.9), channel_id=1, source_target_pairs={{1,0},{2,1},{3,2},{4,3},{5,4},{6,5},{7,6},{8,7},{9,8},{10,9},{11,1... | collective-permute-start | bytes 1572872 | tf_op jit(solution)/shard_map/ppermute | solution.py:34
  32.9 3.9 convolution_bitcast_fusion.9
  53.1 7.0 %collective-permute-start.5 = (bf16[1,32,8192]{2,1,0:T(8,128)(2,1)S(1)}, bf16[1,32,8192]{2,1,0:T(8,128)(2,1)}, u32[]{:S(2)}, u32[]{:S(2)}) collective-permute-start(bf16[1,32,8192]{2,1,0:T(8,128)(2,1)S(1)} %fusion.8), channel_id=1, source_target_pairs={{1,0},{2,1},{3,2},{4,3},{5,4},{6,5},{7,6},{8,7},{9,8},{10,9},{11,1... | collective-permute-start | bytes 1572872 | tf_op jit(solution)/shard_map/ppermute | solution.py:34
  62.5 7.8 %all-to-all-start = ((f32[16,256,128]{2,0,1:T(8,128)}), f32[16,256,128]{2,0,1:T(8,128)}, u32[]{:S(2)}, u32[]{:S(2)}) async-start(f32[16,256,128]{2,0,1:T(8,128)} %copy.60), calls=%async_computation | async-start | bytes 4194304 | tf_op jit(solution)/shard_map/all_to_all | solution.py:124
  80.6 16.0 %all-to-all-done = f32[16,256,128]{2,0,1:T(8,128)} async-done(((f32[16,256,128]{2,0,1:T(8,128)}), f32[16,256,128]{2,0,1:T(8,128)}, u32[]{:S(2)}, u32[]{:S(2)}) %all-to-all-start) | async-done | bytes 2097184 | tf_op jit(solution)/shard_map/all_to_all | solution.py:124
  98.8 4.5 convolution_bitcast_fusion.8
  105.4 5.2 all-to-all-start.1
  120.5 38.9 %all-to-all-done.1 = f32[32,1,128,128]{2,3,1,0:T(8,128)} async-done(((f32[32,1,128,128]{2,3,1,0:T(8,128)}), f32[32,1,128,128]{2,3,1,0:T(8,128)}, u32[]{:S(2)}, u32[]{:S(2)}) %all-to-all-start.1) | async-done | bytes 2097184 | tf_op jit(solution)/shard_map/all_to_all | solution.py:52
  161.4 54.2 %all_to_all.115 = f32[32,1,128,128]{2,3,1,0:T(8,128)S(1)} all-to-all(f32[32,1,128,128]{2,3,1,0:T(8,128)S(1)} %broadcast_in_dim.52), channel_id=1, replica_groups=mesh['slab_0'=4,'slab_1'=2,'coil_0'=4,'coil_1'=8] {'coil_0','coil_1'}, dimensions={0} | all-to-all | bytes 4194304 | tf_op jit(solution)/shard_map/all_to_all | solution.py:64
  224.3 34.5 %all_to_all.116 = f32[32,128,128]{2,0,1:T(8,128)S(1)} all-to-all(f32[32,128,128]{2,0,1:T(8,128)} %copy.87), channel_id=1, replica_groups=mesh['slab_0'=4,'slab_1'=2,'coil_0'=4,'coil_1'=8] {'slab_0','slab_1'}, dimensions={1} | all-to-all | bytes 4194304 | tf_op jit(solution)/shard_map/all_to_all | solution.py:124
  260.0 7.2 %convolution_bitcast_fusion.6 = f32[16,512,128]{1,2,0:T(8,128)S(1)} fusion(f32[256,16,128]{2,1,0:T(8,128)S(1)} %bitcast.389, f32[256,256]{1,0:T(8,128)S(1)} %get-tuple-element.165, f32[256,256]{1,0:T(8,128)S(1)} %get-tuple-element.166), kind=kOutput, calls=%fused_computation.56 | convolution fusion | flops 3221487616 | bytes 6815744 | tf_op jit(solution)/shard_map/ky,yzn->zkn/dot_general | solution.py:136
  267.5 4.2 convolution_bitcast_fusion.5
  276.7 30.7 %all_to_all.117 = f32[16,256,128]{2,0,1:T(8,128)S(1)} all-to-all(f32[16,256,128]{2,0,1:T(8,128)} %copy.91), channel_id=1, replica_groups=mesh['slab_0'=4,'slab_1'=2,'coil_0'=4,'coil_1'=8] {'slab_0','slab_1'}, dimensions={1} | all-to-all | bytes 4194304 | tf_op jit(solution)/shard_map/all_to_all | solution.py:124
  308.0 4.5 convolution_bitcast_fusion.4
  313.2 52.1 %all_to_all.118 = f32[32,1,128,128]{2,3,1,0:T(8,128)S(1)} all-to-all(f32[32,1,128,128]{2,3,1,0:T(8,128)S(1)} %maximum_bitcast_fusion.1), channel_id=1, replica_groups=mesh['slab_0'=4,'slab_1'=2,'coil_0'=4,'coil_1'=8] {'coil_0','coil_1'}, dimensions={0} | all-to-all | bytes 4194304 | tf_op jit(solution)/shard_map/all_to_all | solution.py:52
  366.0 7.5 %all-reduce.8 = (f32[]{:T(128)}, f32[]{:T(128)}) all-reduce(f32[]{:T(128)} %get-tuple-element.7, f32[]{:T(128)} %get-tuple-element.6), channel_id=1, replica_groups=mesh['slab_0'=4,'slab_1'=2,'coil_0'=4,'coil_1'=8] {'slab_0'}, use_global_device_ids=true, to_apply=%region_2.3 | all-reduce | flops 2 | bytes 16 | tf_op jit(solution)/shard_map/psum | solution.py:21
  373.5 9.3 %all-reduce.10 = (f32[]{:T(128)}, f32[]{:T(128)}) all-reduce(f32[]{:T(128)} %get-tuple-element.18, f32[]{:T(128)} %get-tuple-element.19), channel_id=1, replica_groups=mesh['slab_0'=4,'slab_1'=2,'coil_0'=4,'coil_1'=8] {'slab_1'}, use_global_device_ids=true, to_apply=%region_3.4 | all-reduce | flops 2 | bytes 16 | tf_op jit(solution)/shard_map/psum | solution.py:21
  382.8 7.1 %all-reduce.6 = (f32[]{:T(128)}, f32[]{:T(128)}) all-reduce(f32[]{:T(128)} %get-tuple-element.22, f32[]{:T(128)} %get-tuple-element.23), channel_id=1, replica_groups=mesh['slab_0'=4,'slab_1'=2,'coil_0'=4,'coil_1'=8] {'coil_0'}, use_global_device_ids=true, to_apply=%region_4.5 | all-reduce | flops 2 | bytes 16 | tf_op jit(solution)/shard_map/psum | solution.py:21
  390.0 12.9 %all-reduce.4 = (f32[]{:T(128)}, f32[]{:T(128)}) all-reduce(f32[]{:T(128)} %get-tuple-element.14, f32[]{:T(128)} %get-tuple-element.15), channel_id=1, replica_groups=mesh['slab_0'=4,'slab_1'=2,'coil_0'=4,'coil_1'=8] {'coil_1'}, use_global_device_ids=true, to_apply=%region_5.6 | all-reduce | flops 2 | bytes 16 | tf_op jit(solution)/shard_map/psum | solution.py:21
  404.5 47.1 %all_to_all.119 = f32[32,1,128,128]{2,3,1,0:T(8,128)S(1)} all-to-all(f32[32,1,128,128]{2,3,1,0:T(8,128)S(1)} %broadcast_in_dim.53), channel_id=1, replica_groups=mesh['slab_0'=4,'slab_1'=2,'coil_0'=4,'coil_1'=8] {'coil_0','coil_1'}, dimensions={0} | all-to-all | bytes 4194304 | tf_op jit(solution)/shard_map/all_to_all | solution.py:64
  460.3 38.6 %all_to_all.120 = f32[32,128,128]{2,0,1:T(8,128)S(1)} all-to-all(f32[32,128,128]{2,0,1:T(8,128)} %copy.97), channel_id=1, replica_groups=mesh['slab_0'=4,'slab_1'=2,'coil_0'=4,'coil_1'=8] {'slab_0','slab_1'}, dimensions={1} | all-to-all | bytes 4194304 | tf_op jit(solution)/shard_map/all_to_all | solution.py:124
  500.1 7.2 %convolution_bitcast_fusion.2 = f32[16,512,128]{1,2,0:T(8,128)S(1)} fusion(f32[256,16,128]{2,1,0:T(8,128)S(1)} %bitcast.392, f32[256,256]{1,0:T(8,128)S(1)} %get-tuple-element.165, f32[256,256]{1,0:T(8,128)S(1)} %get-tuple-element.166), kind=kOutput, calls=%fused_computation.52 | convolution fusion | flops 3221487616 | bytes 6815744 | tf_op jit(solution)/shard_map/ky,yzn->zkn/dot_general | solution.py:136
  507.7 4.0 convolution_bitcast_fusion.1
  516.6 30.7 %all_to_all.121 = f32[16,256,128]{2,0,1:T(8,128)S(1)} all-to-all(f32[16,256,128]{2,0,1:T(8,128)} %copy.101), channel_id=1, replica_groups=mesh['slab_0'=4,'slab_1'=2,'coil_0'=4,'coil_1'=8] {'slab_0','slab_1'}, dimensions={1} | all-to-all | bytes 4194304 | tf_op jit(solution)/shard_map/all_to_all | solution.py:124
  547.9 4.5 convolution_bitcast_fusion
  553.1 53.2 %all_to_all.122 = f32[32,1,128,128]{2,3,1,0:T(8,128)S(1)} all-to-all(f32[32,1,128,128]{2,3,1,0:T(8,128)S(1)} %maximum_bitcast_fusion.2), channel_id=1, replica_groups=mesh['slab_0'=4,'slab_1'=2,'coil_0'=4,'coil_1'=8] {'coil_0','coil_1'}, dimensions={0} | all-to-all | bytes 4194304 | tf_op jit(solution)/shard_map/all_to_all | solution.py:52
  607.1 7.5 %all-reduce.7 = (f32[]{:T(128)}, f32[]{:T(128)}) all-reduce(f32[]{:T(128)} %get-tuple-element.5, f32[]{:T(128)} %get-tuple-element.4), channel_id=1, replica_groups=mesh['slab_0'=4,'slab_1'=2,'coil_0'=4,'coil_1'=8] {'slab_0'}, use_global_device_ids=true, to_apply=%region_13.14 | all-reduce | flops 2 | bytes 16 | tf_op jit(solution)/shard_map/psum | solution.py:21
  614.6 9.4 %all-reduce.9 = (f32[]{:T(128)}, f32[]{:T(128)}) all-reduce(f32[]{:T(128)} %get-tuple-element.16, f32[]{:T(128)} %get-tuple-element.17), channel_id=1, replica_groups=mesh['slab_0'=4,'slab_1'=2,'coil_0'=4,'coil_1'=8] {'slab_1'}, use_global_device_ids=true, to_apply=%region_14.15 | all-reduce | flops 2 | bytes 16 | tf_op jit(solution)/shard_map/psum | solution.py:21
  624.0 7.2 %all-reduce.5 = (f32[]{:T(128)}, f32[]{:T(128)}) all-reduce(f32[]{:T(128)} %get-tuple-element.20, f32[]{:T(128)} %get-tuple-element.21), channel_id=1, replica_groups=mesh['slab_0'=4,'slab_1'=2,'coil_0'=4,'coil_1'=8] {'coil_0'}, use_global_device_ids=true, to_apply=%region_15.16 | all-reduce | flops 2 | bytes 16 | tf_op jit(solution)/shard_map/psum | solution.py:21
  631.2 13.0 %all-reduce.3 = (f32[]{:T(128)}, f32[]{:T(128)}) all-reduce(f32[]{:T(128)} %get-tuple-element.12, f32[]{:T(128)} %get-tuple-element.13), channel_id=1, replica_groups=mesh['slab_0'=4,'slab_1'=2,'coil_0'=4,'coil_1'=8] {'coil_1'}, use_global_device_ids=true, to_apply=%region_16.17 | all-reduce | flops 2 | bytes 16 | tf_op jit(solution)/shard_map/psum | solution.py:21
  (216 shorter events, 92.2 us)
Async XLA Ops:
  1.8 14.3 %collective-permute-start = (bf16[1,2,8192]{2,1,0:T(2,128)(2,1)S(1)}, bf16[1,2,8192]{2,1,0:T(2,128)(2,1)S(1)}, u32[]{:S(2)}, u32[]{:S(2)}) collective-permute-start(bf16[1,2,8192]{2,1,0:T(2,128)(2,1)S(1)} %pad_maximum_fusion.5), channel_id=1, source_target_pairs={{0,1},{1,2},{2,3},{3,4},{4,5},{5,6},{6,7},{7,8},{8,9},{9,10},{10,1... | collective-permute-start | bytes 98312 | tf_op jit(solution)/shard_map/ppermute | solution.py:33
  6.2 9.9 %collective-permute-start.1 = (bf16[1,2,8192]{2,1,0:T(2,128)(2,1)S(1)}, bf16[1,2,8192]{2,1,0:T(2,128)(2,1)S(1)}, u32[]{:S(2)}, u32[]{:S(2)}) collective-permute-start(bf16[1,2,8192]{2,1,0:T(2,128)(2,1)S(1)} %pad_maximum_fusion.5), channel_id=1, source_target_pairs={{1,0},{2,1},{3,2},{4,3},{5,4},{6,5},{7,6},{8,7},{9,8},{10,9},{11,1... | collective-permute-start | bytes 98312 | tf_op jit(solution)/shard_map/ppermute | solution.py:34
  19.9 10.4 %copy-start.23 = (bf16[3,3,3,32,32]{4,3,2,1,0:T(8,128)(2,1)S(1)}, bf16[3,3,3,32,32]{4,3,2,1,0:T(8,128)(2,1)}, u32[]{:S(2)}) copy-start(bf16[3,3,3,32,32]{4,3,2,1,0:T(8,128)(2,1)} %param.16) | copy-start | bytes 165892
  19.9 11.4 %copy-start.24 = (s32[16,256]{1,0:T(8,128)S(1)}, s32[16,256]{1,0:T(8,128)}, u32[]{:S(2)}) copy-start(s32[16,256]{1,0:T(8,128)} %param.13) | copy-start | bytes 49156
  19.9 11.4 %copy-start = (bf16[1,16,256,128]{3,2,1,0:T(8,128)(2,1)S(1)}, bf16[1,16,256,128]{3,2,1,0:T(8,128)(2,1)}, u32[]{:S(2)}) copy-start(bf16[1,16,256,128]{3,2,1,0:T(8,128)(2,1)} %param.12) | copy-start | bytes 3145732
  20.6 19.7 %collective-permute-start.2 = (bf16[1,32,8192]{2,1,0:T(8,128)(2,1)S(1)}, bf16[1,32,8192]{2,1,0:T(8,128)(2,1)}, u32[]{:S(2)}, u32[]{:S(2)}) collective-permute-start(bf16[1,32,8192]{2,1,0:T(8,128)(2,1)S(1)} %fusion.9), channel_id=1, source_target_pairs={{0,1},{1,2},{2,3},{3,4},{4,5},{5,6},{6,7},{7,8},{8,9},{9,10},{10,1... | collective-permute-start | bytes 1572872 | tf_op jit(solution)/shard_map/ppermute | solution.py:33
  22.6 17.8 %collective-permute-start.3 = (bf16[1,32,8192]{2,1,0:T(8,128)(2,1)S(1)}, bf16[1,32,8192]{2,1,0:T(8,128)(2,1)}, u32[]{:S(2)}, u32[]{:S(2)}) collective-permute-start(bf16[1,32,8192]{2,1,0:T(8,128)(2,1)S(1)} %fusion.9), channel_id=1, source_target_pairs={{1,0},{2,1},{3,2},{4,3},{5,4},{6,5},{7,6},{8,7},{9,8},{10,9},{11,1... | collective-permute-start | bytes 1572872 | tf_op jit(solution)/shard_map/ppermute | solution.py:34
  49.1 1.4 copy-start.27
  50.9 9.4 %copy-start.20 = (bf16[1,32,8192]{2,1,0:T(8,128)(2,1)}, bf16[1,32,8192]{2,1,0:T(8,128)(2,1)S(1)}, u32[]{:S(2)}) copy-start(bf16[1,32,8192]{2,1,0:T(8,128)(2,1)S(1)} %fusion.8) | copy-start | bytes 1572868
  50.9 21.3 %collective-permute-start.4 = (bf16[1,32,8192]{2,1,0:T(8,128)(2,1)S(1)}, bf16[1,32,8192]{2,1,0:T(8,128)(2,1)}, u32[]{:S(2)}, u32[]{:S(2)}) collective-permute-start(bf16[1,32,8192]{2,1,0:T(8,128)(2,1)S(1)} %fusion.8), channel_id=1, source_target_pairs={{0,1},{1,2},{2,3},{3,4},{4,5},{5,6},{6,7},{7,8},{8,9},{9,10},{10,1... | collective-permute-start | bytes 1572872 | tf_op jit(solution)/shard_map/ppermute | solution.py:33
  53.1 19.2 %collective-permute-start.5 = (bf16[1,32,8192]{2,1,0:T(8,128)(2,1)S(1)}, bf16[1,32,8192]{2,1,0:T(8,128)(2,1)}, u32[]{:S(2)}, u32[]{:S(2)}) collective-permute-start(bf16[1,32,8192]{2,1,0:T(8,128)(2,1)S(1)} %fusion.8), channel_id=1, source_target_pairs={{1,0},{2,1},{3,2},{4,3},{5,4},{6,5},{7,6},{8,7},{9,8},{10,9},{11,1... | collective-permute-start | bytes 1572872 | tf_op jit(solution)/shard_map/ppermute | solution.py:34
  62.5 7.8 %copy-start.22 = (f32[1,128,128]{2,1,0:T(8,128)S(1)}, f32[1,128,128]{2,1,0:T(8,128)}, u32[]{:S(2)}) copy-start(f32[1,128,128]{2,1,0:T(8,128)} %param.10) | copy-start | bytes 196612
  62.5 7.9 %copy-start.25 = (bf16[3,3,3,2,32]{4,3,2,1,0:T(2,128)(2,1)S(1)}, bf16[3,3,3,2,32]{4,3,2,1,0:T(2,128)(2,1)}, u32[]{:S(2)}) copy-start(bf16[3,3,3,2,32]{4,3,2,1,0:T(2,128)(2,1)} %param.18) | copy-start | bytes 10372
  62.5 8.8 %copy-start.1 = (bf16[1,32,128,128]{3,2,1,0:T(8,128)(2,1)S(1)}, bf16[1,32,128,128]{3,2,1,0:T(8,128)(2,1)}, u32[]{:S(2)}) copy-start(bf16[1,32,128,128]{3,2,1,0:T(8,128)(2,1)} %param.11) | copy-start | bytes 3145732
  62.5 34.1 %all-to-all-start = ((f32[16,256,128]{2,0,1:T(8,128)}), f32[16,256,128]{2,0,1:T(8,128)}, u32[]{:S(2)}, u32[]{:S(2)}) async-start(f32[16,256,128]{2,0,1:T(8,128)} %copy.60), calls=%async_computation | async-start | bytes 4194304 | tf_op jit(solution)/shard_map/all_to_all | solution.py:124
  105.4 54.0 %all-to-all-start.1 = ((f32[32,1,128,128]{2,3,1,0:T(8,128)}), f32[32,1,128,128]{2,3,1,0:T(8,128)}, u32[]{:S(2)}, u32[]{:S(2)}) async-start(f32[32,1,128,128]{2,3,1,0:T(8,128)} %maximum_bitcast_fusion), calls=%async_computation.1 | async-start | bytes 4194304 | tf_op jit(solution)/shard_map/all_to_all | solution.py:52
  110.6 1.2 copy-start.19
  111.5 1.2 copy-start.18
  112.1 2.1 copy-start.12
  112.1 2.1 copy-start.17
  114.1 1.2 copy-start.15
  114.5 1.2 copy-start.8
  114.5 1.3 copy-start.13
  114.5 1.4 copy-start.21
  115.7 1.3 copy-start.11
  116.3 1.1 copy-start.5
  116.3 1.3 copy-start.9
  117.3 1.1 copy-start.3
  117.3 1.3 copy-start.7
  117.9 2.0 copy-start.2
  117.9 2.0 copy-start.4
  117.9 2.0 copy-start.28
  (5 other events, 5.1 us)
where the time goes:
time: 660 us; the launch traced here: 651 us
  blocking collectives  415 us (63%)
  matrix products  60.3 us (9%)
  waiting for transfers between devices  58.5 us (9%)
  starting transfers between devices  44.9 us (7%)
  local copies, waits for them, and re-layouts  41.3 us (6%)
  other arithmetic  22.8 us (3%)
  between operations  7.7 us (1%)
    all_to_all x4, blocking collectives, transpose_slab(): return lax.all_to_all(volume, SLAB, split_axis=1, concat_axis=0, tiled=True)  135 us
    all_to_all x2, blocking collectives, summed_on_arrival(): lax.all_to_all(tiles, axis, split_axis=0, concat_axis=0, tiled=True)  105 us
    all_to_all x2, blocking collectives, sent_to_all(): return lax.all_to_all(copies, axis, split_axis=0, concat_axis=0, tiled=True)  101 us
    psum x8, blocking collectives, one_axis_at_a_time(): value = lax.psum(value, axis)  74.1 us
    all_to_all x1, waiting for transfers between devices, summed_on_arrival(): lax.all_to_all(tiles, axis, split_axis=0, concat_axis=0, tiled=True)  38.9 us
    ppermute x3, starting transfers between devices, with_halo(): lax.ppermute(initial, axis, [(b, a) for a, b in up])  23.5 us
    all_to_all x1, waiting for transfers between devices, transpose_slab(): return lax.all_to_all(volume, SLAB, split_axis=1, concat_axis=0, tiled=True)  16 us
    dot_general x2, matrix products, through_kspace(): jnp.einsum('ky,yzn->zkn', y_table, moved, precision=highest, preferred_el...  14.3 us
  transfers between devices with their start and end apart: 8, of which 3 were waited for; matrix products, arithmetic and copies ran while one was open for 4% of the time, Pallas kernels for 0%

commit v1 on v0

v1 whole, which is shorter than its diff:
```python
import functools

import jax
import jax.numpy as jnp
import numpy as np
from jax import lax
from jax.experimental import pallas as pl
from jax.experimental.pallas import tpu as pltpu
from jax.sharding import Mesh
from jax.sharding import PartitionSpec as P

AXES = ("x", "k", "y", "g", "b")
SIZES = (4, 2, 4, 4, 2)
GROUP = ("x", "k", "y", "b")
ALL = ("x", "k", "y", "g", "b")

penalty = 0.5
f32 = jnp.float32
bf16 = jnp.bfloat16


def with_halo(value, width):
    count, length = 256, value.shape[0]
    up = [(i, (i + 1) % count) for i in range(count - 1)]
    last = lax.slice_in_dim(value, length - width, length, axis=0)
    initial = lax.slice_in_dim(value, 0, width, axis=0)
    low = lax.ppermute(last, ALL, up)
    high = lax.ppermute(initial, ALL, [(b, a) for a, b in up])
    return jnp.concatenate([low, value, high], axis=0)


def convolve_layer(features, weights, offsets, readout):
    row_total = features.shape[0]
    in_channels = features.shape[1]
    span_cells = features.shape[2]
    out_channels = weights.shape[3]
    extended = with_halo(features, 1)
    padded = jnp.pad(extended, ((0, 0), (0, 0), (readout + 1, readout + 1)))
    column = (jnp.arange(padded.shape[2], dtype=jnp.int32) - 1) % readout
    zero_value = jnp.zeros((), padded.dtype)
    sources = (
        jnp.where(column != readout - 1, padded, zero_value),
        padded,
        jnp.where(column != 0, padded, zero_value),
    )
    running = jnp.zeros((row_total, out_channels, span_cells), jnp.float32)
    for row_shift in range(3):
        for plane_shift in range(3):
            pieces = []
            for column_shift in range(3):
                first_cell = plane_shift * readout + column_shift
                pieces.append(
                    lax.slice(
                        sources[column_shift],
                        (row_shift, 0, first_cell),
                        (row_shift + row_total, in_channels, first_cell + span_cells),
                    )
                )
            stacked = jnp.concatenate(pieces, axis=1)
            kernel = jnp.transpose(weights[row_shift, plane_shift], (1, 0, 2)).reshape(
                out_channels, 3 * in_channels
            )
            running = running + jnp.einsum(
                "oc,ycn->yon", kernel, stacked, preferred_element_type=jnp.float32
            )
    return running + offsets[None, :, None]


def split_table(table):
    table = table.astype(np.float32)
    high = table.astype(jnp.bfloat16)
    low = (table - high.astype(np.float32)).astype(jnp.bfloat16)
    return np.stack([high, low])


def row_order():
    order = np.zeros(256, np.int64)
    for g in range(4):
        for s in range(8):
            for y in range(4):
                for b in range(2):
                    order[g * 64 + s * 8 + y * 2 + b] = s * 32 + y * 8 + 2 * g + b
    return order


def tables():
    rows = row_order()
    angle = 2 * np.pi * (np.outer(np.arange(256), rows) % 256) / 256
    c, s = np.cos(angle) / 16.0, np.sin(angle) / 16.0
    forward = split_table(np.block([[c, s], [-s, c]]))
    backward = split_table(np.block([[c.T, -s.T], [s.T, c.T]]))
    angle = 2 * np.pi * (np.outer(np.arange(128), np.arange(128)) % 128) / 128
    c, s = np.cos(angle) / np.sqrt(128.0), np.sin(angle) / np.sqrt(128.0)
    z_forward = split_table(np.block([[c, -s], [s, c]]))
    z_backward = split_table(np.block([[c, s], [-s, c]]))
    return forward, backward, z_forward, z_backward


def halves(value):
    high = value.astype(bf16)
    low = (value - high.astype(f32)).astype(bf16)
    return high, low


def mm(a, b):
    return jnp.dot(a, b, preferred_element_type=f32)


def table_right(value, table):
    high, low = halves(value)
    return mm(high, table[0]) + (mm(high, table[1]) + mm(low, table[0]))


def table_left(table, value):
    high, low = halves(value)
    return mm(table[0], high) + (mm(table[1], high) + mm(table[0], low))


def to_rows(value):
    first, second = value[:256], value[256:]
    return jnp.concatenate(
        [
            jnp.concatenate([first[:, :128], second[:, :128]], axis=1),
            jnp.concatenate([first[:, 128:], second[:, 128:]], axis=1),
        ],
        axis=0,
    )


def to_lanes(value):
    real, imag = value[:256], value[256:]
    return jnp.concatenate(
        [
            jnp.concatenate([real[:, :128], imag[:, :128]], axis=1),
            jnp.concatenate([real[:, 128:], imag[:, 128:]], axis=1),
        ],
        axis=0,
    )


def folded(value):
    return value.reshape(-1, 8, 128).sum(axis=0)


def cg_kernel(
    den_ref,
    k_ref,
    s_ref,
    mask_ref,
    fy_ref,
    gy_ref,
    fz_ref,
    gz_ref,
    sol_ref,
    res_ref,
    acc,
    mask_all,
    mask_t,
    parts,
    own,
    full,
    stat_a,
    stat_b,
    stat_c,
    stat_own,
    send_sem,
    part_sem,
    full_sem,
    mask_sem,
    stat_sem_a,
    stat_sem_b,
    stat_sem_c,
):
    x, k, y, g, b = (lax.axis_index(name) for name in AXES)
    slab = x * 2 + k
    line = g * 2 + b

    def slab_peer(i):
        t = lax.rem(slab + i, 8)
        return t, {"x": t // 2, "k": lax.rem(t, 2)}

    def y_peer(i):
        t = lax.rem(y + i, 4)
        return t, {"y": t}

    def line_peer(i):
        t = lax.rem(line + i, 8)
        return t, {"g": t // 2, "b": lax.rem(t, 2)}

    def g_peer(i):
        t = lax.rem(g + i, 4)
        return t, {"g": t}

    barrier = pltpu.get_barrier_semaphore()
    for count, peer in ((8, slab_peer), (4, y_peer), (8, line_peer)):
        for i in range(1, count):
            pl.semaphore_signal(
                barrier, inc=1, device_id=peer(i)[1], device_id_type=pl.DeviceIdType.MESH
            )
    pl.semaphore_wait(barrier, 17)

    def send(source, target, slot, arrival, device):
        copy = pltpu.make_async_remote_copy(
            src_ref=source,
            dst_ref=target,
            send_sem=send_sem.at[slot],
            recv_sem=arrival,
            device_id=device,
            device_id_type=pl.DeviceIdType.MESH,
        )
        copy.start()
        return copy

    mask_copies = []
    for i in range(1, 8):
        mask_copies.append(
            send(mask_ref, mask_all.at[slab], i - 1, mask_sem.at[i - 1], slab_peer(i)[1])
        )
    mask_all[pl.ds(slab, 1)] = mask_ref[...][None]

    acc[...] = jnp.zeros_like(acc)

    def maps_of(j):
        return s_ref[j, 0].astype(f32), s_ref[j, 1].astype(f32)

    def add_image(image, pair):
        for n in range(2):
            real, imag = maps_of(2 * pair + n)
            a_real = image[256 * n : 256 * n + 256, :128]
            a_imag = image[256 * n : 256 * n + 256, 128:]
            acc[0] += real * a_real + imag * a_imag
            acc[1] += real * a_imag - imag * a_real

    def adjoint_pair(pair, _):
        planes = []
        for n in range(2):
            j = 2 * pair + n
            planes.append(
                jnp.concatenate(
                    [k_ref[:, j, 0].reshape(128, 256), k_ref[:, j, 1].reshape(128, 256)], axis=1
                )
            )
        spectrum = jnp.concatenate(planes, axis=0)
        dims = (((1,), (1,)), ((), ()))
        rows = lax.dot_general(
            gy_ref[0], spectrum, dims, preferred_element_type=f32
        ) + lax.dot_general(gy_ref[1], spectrum, dims, preferred_element_type=f32)
        add_image(table_right(to_lanes(rows), gz_ref), pair)
        return 0

    lax.fori_loop(0, 4, adjoint_pair, 0)

    def reduce_scatter(step):
        copies = []
        for i in range(1, 4):
            t, device = g_peer(i)
            first = pl.multiple_of(t * 64, 64)
            copies.append(
                send(
                    acc.at[:, pl.ds(first, 64)],
                    parts.at[step, i - 1],
                    14 + i,
                    part_sem.at[step, i - 1],
                    device,
                )
            )
        mine = acc[:, pl.ds(pl.multiple_of(g * 64, 64), 64)]

        def finish():
            for copy in copies:
                copy.wait()
            return mine + ((parts[step, 0] + parts[step, 1]) + parts[step, 2])

        return finish

    def gather(step, value):
        mine = pl.ds(pl.multiple_of(g * 64, 64), 64)
        own[step] = value
        full[step, :, mine] = value
        copies = []
        for i in range(1, 4):
            _, device = g_peer(i)
            copies.append(
                send(
                    own.at[step],
                    full.at[step, :, mine],
                    14 + i,
                    full_sem.at[step, i - 1],
                    device,
                )
            )
        return copies

    right = reduce_scatter(0)() + penalty * den_ref[...]
    gathers = gather(0, right)
    for copy in mask_copies:
        copy.wait_recv()
    eye = (
        lax.broadcasted_iota(jnp.int32, (256, 256), 0)
        == lax.broadcasted_iota(jnp.int32, (256, 256), 1)
    ).astype(bf16)
    mask_t[...] = lax.dot_general(
        eye, mask_all[...].reshape(128, 256), (((1,), (1,)), ((), ())), preferred_element_type=f32
    )

    def operator(step):
        acc[...] = jnp.zeros_like(acc)

        def one_pair(pair, energy):
            d_real, d_imag = full[step, 0], full[step, 1]
            pieces = []
            for n in range(2):
                real, imag = maps_of(2 * pair + n)
                pieces.append(
                    jnp.concatenate(
                        [real * d_real - imag * d_imag, real * d_imag + imag * d_real], axis=1
                    )
                )
            spectrum = to_rows(table_right(jnp.concatenate(pieces, axis=0), fz_ref))
            mask = mask_t[...]
            mask = jnp.concatenate([mask, mask], axis=1)
            mask = jnp.concatenate([mask, mask], axis=0)
            spectrum = table_left(fy_ref, spectrum) * mask
            squares = spectrum * spectrum
            energy = energy + folded(squares[:, :128] + squares[:, 128:])
            image = to_lanes(table_left(gy_ref, spectrum))
            add_image(table_right(image, gz_ref), pair)
            return energy

        return lax.fori_loop(0, 4, one_pair, jnp.zeros((8, 128), f32))

    def totals(step, norm, energy):
        value = jnp.stack([norm, energy])
        stages = (
            (8, slab_peer, slab, stat_a, stat_sem_a),
            (4, y_peer, y, stat_b, stat_sem_b),
            (8, line_peer, line, stat_c, stat_sem_c),
        )
        for stage, (count, peer, me, slots, sems) in enumerate(stages):
            stat_own[step, stage] = value
            slots[step, pl.ds(me, 1)] = value[None]
            copies = []
            for i in range(1, count):
                copies.append(
                    send(
                        stat_own.at[step, stage],
                        slots.at[step, me],
                        7 + i,
                        sems.at[step, i - 1],
                        peer(i)[1],
                    )
                )
            for copy in copies:
                copy.wait()
            value = slots[step, 0]
            for i in range(1, count):
                value = value + slots[step, i]
        return jnp.sum(value[0]), jnp.sum(value[1])

    def norm_of(value):
        return folded((value * value).reshape(128, 128))

    for copy in mask_copies:
        copy.wait_send()

    for copy in gathers:
        copy.wait()
    energy = operator(0)
    finish = reduce_scatter(1)
    rr, energy = totals(0, norm_of(right), energy)
    alpha = rr / (energy + penalty * rr)
    image = finish() + penalty * right
    residual = right - alpha * image
    gathers = gather(1, residual)
    for copy in gathers:
        copy.wait()
    energy = operator(1)
    finish = reduce_scatter(2)
    fresh, energy = totals(1, norm_of(residual), energy)
    growth = fresh / rr
    step_size = fresh / (energy + penalty * fresh - growth * fresh / alpha)
    q = finish() + penalty * residual + growth * image
    sol_ref[...] = alpha * right + step_size * (residual + growth * right)
    res_ref[...] = residual - step_size * q


def cg(den, spectrum, maps, mask):
    forward, backward, z_forward, z_backward = tables()
    vmem = pl.BlockSpec(memory_space=pltpu.VMEM)
    out = jax.ShapeDtypeStruct((2, 64, 128), f32)
    dma = pltpu.SemaphoreType.DMA
    return pl.pallas_call(
        cg_kernel,
        out_shape=(out, out),
        in_specs=[vmem] * 8,
        out_specs=(vmem, vmem),
        scratch_shapes=[
            pltpu.VMEM((2, 256, 128), f32),
            pltpu.VMEM((8, 16, 256), bf16),
            pltpu.VMEM((256, 128), f32),
            pltpu.VMEM((3, 3, 2, 64, 128), f32),
            pltpu.VMEM((2, 2, 64, 128), f32),
            pltpu.VMEM((2, 2, 256, 128), f32),
            pltpu.VMEM((2, 8, 2, 8, 128), f32),
            pltpu.VMEM((2, 4, 2, 8, 128), f32),
            pltpu.VMEM((2, 8, 2, 8, 128), f32),
            pltpu.VMEM((2, 3, 2, 8, 128), f32),
            dma((18,)),
            dma((3, 3)),
            dma((2, 3)),
            dma((7,)),
            dma((2, 7)),
            dma((2, 3)),
            dma((2, 7)),
        ],
        compiler_params=pltpu.CompilerParams(
            collective_id=0, has_side_effects=True, vmem_limit_bytes=60 * 1024 * 1024
        ),
    )(
        den,
        spectrum,
        maps,
        mask,
        jnp.asarray(forward),
        jnp.asarray(backward),
        jnp.asarray(z_forward),
        jnp.asarray(z_backward),
    )


def body(
    prior_image,
    coil_maps,
    kspace,
    sampling,
    weight_first,
    bias_first,
    weight_middle,
    bias_middle,
    weight_last,
    bias_last,
):
    readout = prior_image.shape[2] // 2
    own_rows = prior_image.shape[0]
    planes = prior_image.shape[1]

    def exchange(value):
        return lax.all_to_all(value, GROUP, split_axis=0, concat_axis=0, tiled=True)

    mask = sampling.astype(bf16)
    measured = kspace[0] * mask[:, :, None]
    spectrum = exchange(measured.reshape(16, 256, 2, 64).transpose(3, 2, 0, 1))
    spectrum = spectrum.reshape(8, 8, 2, 16, 256)
    maps = coil_maps[0].reshape(4, 4, 2, 128, 2, 64).transpose(5, 4, 1, 0, 2, 3)
    maps = exchange(maps.reshape(64, 2, 4, 8, 128))
    maps = maps.reshape(8, 8, 2, 4, 8, 128).transpose(1, 2, 3, 0, 4, 5).reshape(8, 2, 256, 128)

    features = (
        jnp.stack([prior_image[..., :readout], prior_image[..., readout:]], axis=1)
        .reshape(own_rows, 2, planes * readout)
        .astype(jnp.bfloat16)
    )
    hidden = jax.nn.relu(convolve_layer(features, weight_first, bias_first, readout)).astype(
        jnp.bfloat16
    )
    hidden = jax.nn.relu(convolve_layer(hidden, weight_middle, bias_middle, readout)).astype(
        jnp.bfloat16
    )
    output = convolve_layer(hidden, weight_last, bias_last, readout).reshape(
        own_rows, 2, planes, readout
    )
    denoised = prior_image + jnp.concatenate([output[:, 0], output[:, 1]], axis=-1)
    den = exchange(denoised[0].reshape(128, 2, 64).transpose(2, 1, 0)).transpose(1, 0, 2)
    sol, res = cg(den, spectrum, maps, mask)
    both = exchange(jnp.stack([sol, res]).transpose(2, 0, 1, 3))
    both = both.transpose(1, 3, 2, 0).reshape(2, 1, 128, 128)
    return both[0], both[1]


def solution(mesh):
    torus = Mesh(mesh.devices.reshape(SIZES), AXES)
    coil = ("y", "g", "b")
    slab = ("x", "k")
    in_specs = (
        P(ALL, None, None),
        P(coil, slab, None, None),
        P(coil, slab, None, None),
        P(slab, None),
        P(),
        P(),
        P(),
        P(),
        P(),
        P(),
    )
    out_specs = (P(ALL, None, None), P(ALL, None, None))
    return jax.shard_map(body, mesh=torus, in_specs=in_specs, out_specs=out_specs, check_vma=False)
```

time: 660 us -> 242 us (0.37); the launches traced: 651 us -> 241 us
  blocking collectives: 415 us -> 14.7 us
  Pallas kernels: 0 us -> 84.8 us
  matrix products: 60.3 us -> 9.25 us
  local copies, waits for them, and re-layouts: 41.3 us -> 22.1 us
  other arithmetic: 22.8 us -> 4.08 us
    all_to_all x8 -> x1, blocking collectives: 341 us -> 14.7 us  [exchange(): return lax.all_to_all(value, GROUP, split_axis=0, concat_axis=0, tiled=True)]
    pallas_call x0 -> x1, Pallas kernels: none -> 84.8 us  [cg(): pl.pallas_call(cg_kernel, out_shape=(out, out), in_specs=[vmem] * 8, out_...]
    psum x8 -> x0, blocking collectives: 74.1 us -> none  [one_axis_at_a_time(): value = lax.psum(value, axis)]
    dot_general x10 -> x0, matrix products: 46.9 us -> none  [the longest x2 14.3 us: through_kspace(): jnp.einsum('ky,yzn->zkn', y_table, moved, precision=highest, preferred_el...]
    all_to_all x2 -> x3, waiting for transfers between devices: 54.9 us -> 37.2 us  [exchange(): return lax.all_to_all(value, GROUP, split_axis=0, concat_axis=0, tiled=True)]
    concatenate x5 -> x0, local copies, waits for them, and re-layouts: 14.2 us -> none  [combine(): return jnp.concatenate([real_part, imag_part], axis=-1)]
    ppermute x6, waiting for transfers between devices: 3.58 us -> 16.8 us  [the longest x3 15.9 us: with_halo(): low = lax.ppermute(last, ALL, up)]
    all_to_all x2 -> x3, starting transfers between devices: 13 us -> 19 us  [exchange(): return lax.all_to_all(value, GROUP, split_axis=0, concat_axis=0, tiled=True)]
  transfers between devices with their start and end apart: 8 -> 9, of which waited for: 3 -> 6; matrix products, arithmetic and copies ran while one was open for 4% -> 4% of each run, Pallas kernels for 0% -> 0%
where the time goes in v1:
time: 242 us; the launch traced here: 241 us
  Pallas kernels  84.8 us (35%)
  waiting for transfers between devices  54 us (22%)
  starting transfers between devices  50.8 us (21%)
  local copies, waits for them, and re-layouts  22.1 us (9%)
  blocking collectives  14.7 us (6%)
  matrix products  9.25 us (4%)
  other arithmetic  4.08 us (2%)
    pallas_call x1, Pallas kernels, cg(): pl.pallas_call(cg_kernel, out_shape=(out, out), in_specs=[vmem] * 8, out_...  84.8 us
    all_to_all x3, waiting for transfers between devices, exchange(): return lax.all_to_all(value, GROUP, split_axis=0, concat_axis=0, tiled=True)  37.2 us
    ppermute x3, starting transfers between devices, with_halo(): high = lax.ppermute(initial, ALL, [(b, a) for a, b in up])  23.5 us
    all_to_all x3, starting transfers between devices, exchange(): return lax.all_to_all(value, GROUP, split_axis=0, concat_axis=0, tiled=True)  19 us
    ppermute x3, waiting for transfers between devices, with_halo(): low = lax.ppermute(last, ALL, up)  15.9 us
    all_to_all x1, blocking collectives, exchange(): return lax.all_to_all(value, GROUP, split_axis=0, concat_axis=0, tiled=True)  14.7 us
    dot_general x27, matrix products, convolve_layer(): jnp.einsum('oc,ycn->yon', kernel, stacked, preferred_element_type=jnp.flo...  9.25 us
    ppermute x3, starting transfers between devices, with_halo(): low = lax.ppermute(last, ALL, up)  8.2 us
  transfers between devices with their start and end apart: 9, of which 6 were waited for; matrix products, arithmetic and copies ran while one was open for 4% of the time, Pallas kernels for 0%

profile of v1, /device:TPU:1, one launch (start us, length us, event | category | flops | bytes accessed | tf_op | source)
XLA Modules:
  0.0 240.8 jit_solution(11793249815360505612)
XLA Ops:
  0.6 0.8 convert.8
  1.8 4.4 %collective-permute-start = (bf16[1,2,8192]{2,1,0:T(2,128)(2,1)S(1)}, bf16[1,2,8192]{2,1,0:T(2,128)(2,1)S(1)}, u32[]{:S(2)}, u32[]{:S(2)}) collective-permute-start(bf16[1,2,8192]{2,1,0:T(2,128)(2,1)S(1)} %pad_maximum_fusion), channel_id=1, source_target_pairs={{0,1},{1,2},{2,3},{3,4},{4,5},{5,6},{6,7},{7,8},{8,9},{9,10},{10,1... | collective-permute-start | bytes 98312 | tf_op jit(solution)/shard_map/ppermute | solution.py:27
  6.2 8.9 %collective-permute-start.1 = (bf16[1,2,8192]{2,1,0:T(2,128)(2,1)S(1)}, bf16[1,2,8192]{2,1,0:T(2,128)(2,1)S(1)}, u32[]{:S(2)}, u32[]{:S(2)}) collective-permute-start(bf16[1,2,8192]{2,1,0:T(2,128)(2,1)S(1)} %pad_maximum_fusion), channel_id=1, source_target_pairs={{1,0},{2,1},{3,2},{4,3},{5,4},{6,5},{7,6},{8,7},{9,8},{10,9},{11,1... | collective-permute-start | bytes 98312 | tf_op jit(solution)/shard_map/ppermute | solution.py:28
  15.1 0.8 slice_bitcast_fusion.20
  20.9 1.9 collective-permute-start.2
  22.8 7.5 %collective-permute-start.3 = (bf16[1,32,8192]{2,1,0:T(8,128)(2,1)S(1)}, bf16[1,32,8192]{2,1,0:T(8,128)(2,1)S(1)}, u32[]{:S(2)}, u32[]{:S(2)}) collective-permute-start(bf16[1,32,8192]{2,1,0:T(8,128)(2,1)S(1)} %fusion.9), channel_id=1, source_target_pairs={{1,0},{2,1},{3,2},{4,3},{5,4},{6,5},{7,6},{8,7},{9,8},{10,9},{11,1... | collective-permute-start | bytes 1572872 | tf_op jit(solution)/shard_map/ppermute | solution.py:28
  31.4 9.1 %collective-permute-done.2 = bf16[1,32,8192]{2,1,0:T(8,128)(2,1)S(1)} collective-permute-done((bf16[1,32,8192]{2,1,0:T(8,128)(2,1)S(1)}, bf16[1,32,8192]{2,1,0:T(8,128)(2,1)S(1)}, u32[]{:S(2)}, u32[]{:S(2)}) %collective-permute-start.2) | collective-permute-done | bytes 524320 | tf_op jit(solution)/shard_map/ppermute | solution.py:27
  41.3 0.9 fusion.171
  42.3 1.4 fusion.172
  43.7 0.8 fusion.170
  48.0 1.9 collective-permute-start.4
  49.9 7.1 %collective-permute-start.5 = (bf16[1,32,8192]{2,1,0:T(8,128)(2,1)S(1)}, bf16[1,32,8192]{2,1,0:T(8,128)(2,1)S(1)}, u32[]{:S(2)}, u32[]{:S(2)}) collective-permute-start(bf16[1,32,8192]{2,1,0:T(8,128)(2,1)S(1)} %fusion.8), channel_id=1, source_target_pairs={{1,0},{2,1},{3,2},{4,3},{5,4},{6,5},{7,6},{8,7},{9,8},{10,9},{11,1... | collective-permute-start | bytes 1572872 | tf_op jit(solution)/shard_map/ppermute | solution.py:28
  58.0 6.8 %collective-permute-done.4 = bf16[1,32,8192]{2,1,0:T(8,128)(2,1)S(1)} collective-permute-done((bf16[1,32,8192]{2,1,0:T(8,128)(2,1)S(1)}, bf16[1,32,8192]{2,1,0:T(8,128)(2,1)S(1)}, u32[]{:S(2)}, u32[]{:S(2)}) %collective-permute-start.4) | collective-permute-done | bytes 524320 | tf_op jit(solution)/shard_map/ppermute | solution.py:27
  64.8 0.9 collective-permute-done.5
  66.5 0.9 fusion.168
  67.4 1.4 fusion.169
  68.8 0.8 fusion.167
  74.3 10.0 %all-to-all-start = ((f32[64,2,128]{2,1,0:T(2,128)}), f32[64,2,128]{2,1,0:T(2,128)S(1)}, u32[]{:S(2)}, u32[]{:S(2)}) async-start(f32[64,2,128]{2,1,0:T(2,128)} %copy.94), calls=%async_computation | async-start | bytes 131072 | tf_op jit(solution)/shard_map/all_to_all | solution.py:448
  85.1 1.7 copy.101
  86.8 5.7 %all-to-all-done = f32[64,2,128]{2,1,0:T(2,128)S(1)} async-done(((f32[64,2,128]{2,1,0:T(2,128)}), f32[64,2,128]{2,1,0:T(2,128)S(1)}, u32[]{:S(2)}, u32[]{:S(2)}) %all-to-all-start) | async-done | bytes 65568 | tf_op jit(solution)/shard_map/all_to_all | solution.py:448
  92.4 4.6 %all-to-all-start.2 = ((bf16[64,2,4,8,128]{4,3,2,1,0:T(8,128)(2,1)}), bf16[64,2,4,8,128]{4,3,2,1,0:T(8,128)(2,1)S(1)}, u32[]{:S(2)}, u32[]{:S(2)}) async-start(bf16[64,2,4,8,128]{4,3,2,1,0:T(8,128)(2,1)} %copy.101), calls=%async_computation.2 | async-start | bytes 2097152 | tf_op jit(solution)/shard_map/all_to_all | solution.py:448
  97.7 2.1 copy.97
  99.8 15.5 %all-to-all-done.2 = bf16[64,2,4,8,128]{4,3,2,1,0:T(8,128)(2,1)S(1)} async-done(((bf16[64,2,4,8,128]{4,3,2,1,0:T(8,128)(2,1)}), bf16[64,2,4,8,128]{4,3,2,1,0:T(8,128)(2,1)S(1)}, u32[]{:S(2)}, u32[]{:S(2)}) %all-to-all-start.2) | async-done | bytes 1048608 | tf_op jit(solution)/shard_map/all_to_all | solution.py:448
  115.3 4.4 %all-to-all-start.1 = ((bf16[64,2,16,256]{3,1,2,0:T(2,128)(2,1)}), bf16[64,2,16,256]{3,1,2,0:T(2,128)(2,1)S(1)}, u32[]{:S(2)}, u32[]{:S(2)}) async-start(bf16[64,2,16,256]{3,1,2,0:T(2,128)(2,1)} %copy.97), calls=%async_computation.1 | async-start | bytes 2097152 | tf_op jit(solution)/shard_map/all_to_all | solution.py:448
  120.3 1.3 copy.102
  121.6 16.0 %all-to-all-done.1 = bf16[64,2,16,256]{3,1,2,0:T(2,128)(2,1)S(1)} async-done(((bf16[64,2,16,256]{3,1,2,0:T(2,128)(2,1)}), bf16[64,2,16,256]{3,1,2,0:T(2,128)(2,1)S(1)}, u32[]{:S(2)}, u32[]{:S(2)}) %all-to-all-start.1) | async-done | bytes 1048608 | tf_op jit(solution)/shard_map/all_to_all | solution.py:448
  137.7 1.2 copy.98
  138.8 84.8 %shard_map.149 = (f32[2,64,128]{2,1,0:T(8,128)}, f32[2,64,128]{2,1,0:T(8,128)}) custom-call(f32[2,64,128]{2,1,0:T(8,128)} %bitcast.304, bf16[8,8,2,16,256]{4,3,2,1,0:T(8,128)(2,1)} %bitcast.302, bf16[8,2,256,128]{3,2,1,0:T(8,128)(2,1)} %bitcast.301, bf16[16,256]{1,0:T(8,128)(2,1)} %copy-done.4, bf16[2,512,512]{2,1,0:T(8,128)(2,1)} %constant.42.clone.fy_ref, ...), custom_call_target="tpu_custom_call" | custom-call | tf_op jit(solution)/shard_map/pallas_call | solution.py:392
  223.7 0.9 maximum_bitcast_fusion.54
  224.7 14.7 %all_to_all.20 = f32[64,2,2,128]{3,2,1,0:T(2,128)S(1)} all-to-all(f32[64,2,2,128]{3,2,1,0:T(2,128)S(1)} %copy.103), channel_id=1, replica_groups=mesh['x'=4,'k'=2,'y'=4,'g'=4,'b'=2] {'x','k','y','b'}, dimensions={0} | all-to-all | bytes 262144 | tf_op jit(solution)/shard_map/all_to_all | solution.py:448
  239.4 0.7 copy.105
  240.1 0.7 copy.106
  (125 shorter events, 18.9 us)
Async XLA Ops:
  1.8 14.3 %collective-permute-start = (bf16[1,2,8192]{2,1,0:T(2,128)(2,1)S(1)}, bf16[1,2,8192]{2,1,0:T(2,128)(2,1)S(1)}, u32[]{:S(2)}, u32[]{:S(2)}) collective-permute-start(bf16[1,2,8192]{2,1,0:T(2,128)(2,1)S(1)} %pad_maximum_fusion), channel_id=1, source_target_pairs={{0,1},{1,2},{2,3},{3,4},{4,5},{5,6},{6,7},{7,8},{8,9},{9,10},{10,1... | collective-permute-start | bytes 98312 | tf_op jit(solution)/shard_map/ppermute | solution.py:27
  6.2 9.9 %collective-permute-start.1 = (bf16[1,2,8192]{2,1,0:T(2,128)(2,1)S(1)}, bf16[1,2,8192]{2,1,0:T(2,128)(2,1)S(1)}, u32[]{:S(2)}, u32[]{:S(2)}) collective-permute-start(bf16[1,2,8192]{2,1,0:T(2,128)(2,1)S(1)} %pad_maximum_fusion), channel_id=1, source_target_pairs={{1,0},{2,1},{3,2},{4,3},{5,4},{6,5},{7,6},{8,7},{9,8},{10,9},{11,1... | collective-permute-start | bytes 98312 | tf_op jit(solution)/shard_map/ppermute | solution.py:28
  19.9 0.7 copy-start.7
  19.9 10.4 %copy-start.3 = (bf16[3,3,3,32,32]{4,3,2,1,0:T(8,128)(2,1)S(1)}, bf16[3,3,3,32,32]{4,3,2,1,0:T(8,128)(2,1)}, u32[]{:S(2)}) copy-start(bf16[3,3,3,32,32]{4,3,2,1,0:T(8,128)(2,1)} %param.20) | copy-start | bytes 165892
  20.9 19.6 %collective-permute-start.2 = (bf16[1,32,8192]{2,1,0:T(8,128)(2,1)S(1)}, bf16[1,32,8192]{2,1,0:T(8,128)(2,1)S(1)}, u32[]{:S(2)}, u32[]{:S(2)}) collective-permute-start(bf16[1,32,8192]{2,1,0:T(8,128)(2,1)S(1)} %fusion.9), channel_id=1, source_target_pairs={{0,1},{1,2},{2,3},{3,4},{4,5},{5,6},{6,7},{7,8},{8,9},{9,10},{10,1... | collective-permute-start | bytes 1572872 | tf_op jit(solution)/shard_map/ppermute | solution.py:27
  22.8 17.7 %collective-permute-start.3 = (bf16[1,32,8192]{2,1,0:T(8,128)(2,1)S(1)}, bf16[1,32,8192]{2,1,0:T(8,128)(2,1)S(1)}, u32[]{:S(2)}, u32[]{:S(2)}) collective-permute-start(bf16[1,32,8192]{2,1,0:T(8,128)(2,1)S(1)} %fusion.9), channel_id=1, source_target_pairs={{1,0},{2,1},{3,2},{4,3},{5,4},{6,5},{7,6},{8,7},{9,8},{10,9},{11,1... | collective-permute-start | bytes 1572872 | tf_op jit(solution)/shard_map/ppermute | solution.py:28
  47.0 0.7 copy-start.8
  47.7 9.4 %copy-start.6 = (bf16[3,3,3,2,32]{4,3,2,1,0:T(2,128)(2,1)S(1)}, bf16[3,3,3,2,32]{4,3,2,1,0:T(2,128)(2,1)}, u32[]{:S(2)}) copy-start(bf16[3,3,3,2,32]{4,3,2,1,0:T(2,128)(2,1)} %param.22) | copy-start | bytes 10372
  48.0 16.7 %collective-permute-start.4 = (bf16[1,32,8192]{2,1,0:T(8,128)(2,1)S(1)}, bf16[1,32,8192]{2,1,0:T(8,128)(2,1)S(1)}, u32[]{:S(2)}, u32[]{:S(2)}) collective-permute-start(bf16[1,32,8192]{2,1,0:T(8,128)(2,1)S(1)} %fusion.8), channel_id=1, source_target_pairs={{0,1},{1,2},{2,3},{3,4},{4,5},{5,6},{6,7},{7,8},{8,9},{9,10},{10,1... | collective-permute-start | bytes 1572872 | tf_op jit(solution)/shard_map/ppermute | solution.py:27
  49.9 15.7 %collective-permute-start.5 = (bf16[1,32,8192]{2,1,0:T(8,128)(2,1)S(1)}, bf16[1,32,8192]{2,1,0:T(8,128)(2,1)S(1)}, u32[]{:S(2)}, u32[]{:S(2)}) collective-permute-start(bf16[1,32,8192]{2,1,0:T(8,128)(2,1)S(1)} %fusion.8), channel_id=1, source_target_pairs={{1,0},{2,1},{3,2},{4,3},{5,4},{6,5},{7,6},{8,7},{9,8},{10,9},{11,1... | collective-permute-start | bytes 1572872 | tf_op jit(solution)/shard_map/ppermute | solution.py:28
  71.9 0.7 copy-start.9
  72.6 0.8 copy-start.2
  72.6 11.7 %copy-start = (bf16[1,32,128,128]{3,2,1,0:T(8,128)(2,1)S(1)}, bf16[1,32,128,128]{3,2,1,0:T(8,128)(2,1)}, u32[]{:S(2)}) copy-start(bf16[1,32,128,128]{3,2,1,0:T(8,128)(2,1)} %param.15) | copy-start | bytes 3145732
  74.3 18.2 %all-to-all-start = ((f32[64,2,128]{2,1,0:T(2,128)}), f32[64,2,128]{2,1,0:T(2,128)S(1)}, u32[]{:S(2)}, u32[]{:S(2)}) async-start(f32[64,2,128]{2,1,0:T(2,128)} %copy.94), calls=%async_computation | async-start | bytes 131072 | tf_op jit(solution)/shard_map/all_to_all | solution.py:448
  85.1 11.9 %copy-start.5 = (s32[16,256]{1,0:T(8,128)S(1)}, s32[16,256]{1,0:T(8,128)}, u32[]{:S(2)}) copy-start(s32[16,256]{1,0:T(8,128)} %param.17) | copy-start | bytes 49156
  85.1 11.9 %copy-start.1 = (bf16[1,16,256,128]{3,2,1,0:T(8,128)(2,1)S(1)}, bf16[1,16,256,128]{3,2,1,0:T(8,128)(2,1)}, u32[]{:S(2)}) copy-start(bf16[1,16,256,128]{3,2,1,0:T(8,128)(2,1)} %param.16) | copy-start | bytes 3145732
  92.4 22.8 %all-to-all-start.2 = ((bf16[64,2,4,8,128]{4,3,2,1,0:T(8,128)(2,1)}), bf16[64,2,4,8,128]{4,3,2,1,0:T(8,128)(2,1)S(1)}, u32[]{:S(2)}, u32[]{:S(2)}) async-start(bf16[64,2,4,8,128]{4,3,2,1,0:T(8,128)(2,1)} %copy.101), calls=%async_computation.2 | async-start | bytes 2097152 | tf_op jit(solution)/shard_map/all_to_all | solution.py:448
  97.0 0.6 copy-start.4
  115.3 22.4 %all-to-all-start.1 = ((bf16[64,2,16,256]{3,1,2,0:T(2,128)(2,1)}), bf16[64,2,16,256]{3,1,2,0:T(2,128)(2,1)S(1)}, u32[]{:S(2)}, u32[]{:S(2)}) async-start(bf16[64,2,16,256]{3,1,2,0:T(2,128)(2,1)} %copy.97), calls=%async_computation.1 | async-start | bytes 2097152 | tf_op jit(solution)/shard_map/all_to_all | solution.py:448

commit v2 on v1

--- a/solution.py
+++ b/solution.py
@@ -17,53 +17,6 @@
 penalty = 0.5
 f32 = jnp.float32
 bf16 = jnp.bfloat16
-
-
-def with_halo(value, width):
-    count, length = 256, value.shape[0]
-    up = [(i, (i + 1) % count) for i in range(count - 1)]
-    last = lax.slice_in_dim(value, length - width, length, axis=0)
-    initial = lax.slice_in_dim(value, 0, width, axis=0)
-    low = lax.ppermute(last, ALL, up)
-    high = lax.ppermute(initial, ALL, [(b, a) for a, b in up])
-    return jnp.concatenate([low, value, high], axis=0)
-
-
-def convolve_layer(features, weights, offsets, readout):
-    row_total = features.shape[0]
-    in_channels = features.shape[1]
-    span_cells = features.shape[2]
-    out_channels = weights.shape[3]
-    extended = with_halo(features, 1)
-    padded = jnp.pad(extended, ((0, 0), (0, 0), (readout + 1, readout + 1)))
-    column = (jnp.arange(padded.shape[2], dtype=jnp.int32) - 1) % readout
-    zero_value = jnp.zeros((), padded.dtype)
-    sources = (
-        jnp.where(column != readout - 1, padded, zero_value),
-        padded,
-        jnp.where(column != 0, padded, zero_value),
-    )
-    running = jnp.zeros((row_total, out_channels, span_cells), jnp.float32)
-    for row_shift in range(3):
-        for plane_shift in range(3):
-            pieces = []
-            for column_shift in range(3):
-                first_cell = plane_shift * readout + column_shift
-                pieces.append(
-                    lax.slice(
-                        sources[column_shift],
-                        (row_shift, 0, first_cell),
-                        (row_shift + row_total, in_channels, first_cell + span_cells),
-                    )
-                )
-            stacked = jnp.concatenate(pieces, axis=1)
-            kernel = jnp.transpose(weights[row_shift, plane_shift], (1, 0, 2)).reshape(
-                out_channels, 3 * in_channels
-            )
-            running = running + jnp.einsum(
-                "oc,ycn->yon", kernel, stacked, preferred_element_type=jnp.float32
-            )
-    return running + offsets[None, :, None]
 
 
 def split_table(table):
@@ -142,17 +95,78 @@
     return value.reshape(-1, 8, 128).sum(axis=0)
 
 
-def cg_kernel(
-    den_ref,
-    k_ref,
-    s_ref,
+def decode_group(i):
+    return {"x": i // 16, "k": lax.rem(i // 8, 2), "y": lax.rem(i // 2, 4), "b": lax.rem(i, 2)}
+
+
+def decode_all(i):
+    return {
+        "x": i // 64,
+        "k": lax.rem(i // 32, 2),
+        "y": lax.rem(i // 8, 4),
+        "g": lax.rem(i // 2, 4),
+        "b": lax.rem(i, 2),
+    }
+
+
+def lanes(shape):
+    return lax.broadcasted_iota(jnp.int32, shape, len(shape) - 1)
+
+
+def plane_shift(value, dz):
+    if dz == 0:
+        return value
+    if dz < 0:
+        edge = pltpu.roll(value[:, -128:], 64, 1)
+        edge = jnp.where(lanes(edge.shape) >= 64, edge, 0.0)
+        return jnp.concatenate([edge, value[:, :-128]], axis=1)
+    edge = pltpu.roll(value[:, :128], 64, 1)
+    edge = jnp.where(lanes(edge.shape) < 64, edge, 0.0)
+    return jnp.concatenate([value[:, 128:], edge], axis=1)
+
+
+def column_shift(value, dx):
+    if dx == 0:
+        return value
+    width = value.shape[1]
+    column = lax.rem(lanes(value.shape), 64)
+    if dx < 0:
+        return jnp.where(column != 0, pltpu.roll(value, 1, 1), 0.0)
+    return jnp.where(column != 63, pltpu.roll(value, width - 1, 1), 0.0)
+
+
+def step_kernel(
+    feat_ref,
+    prior_ref,
+    k_hbm,
+    m_hbm,
     mask_ref,
+    w1_ref,
+    w2_ref,
+    w3_ref,
+    b1_ref,
+    b2_ref,
+    b3_ref,
     fy_ref,
     gy_ref,
     fz_ref,
     gz_ref,
     sol_ref,
     res_ref,
+    k_ref,
+    m_ref,
+    s_ref,
+    fbuf,
+    f_rows,
+    a1,
+    h1m,
+    h1e,
+    p3,
+    dplanes,
+    dsrc,
+    dbuf,
+    osrc,
+    obuf,
     acc,
     mask_all,
     mask_t,
@@ -170,10 +184,24 @@
     stat_sem_a,
     stat_sem_b,
     stat_sem_c,
+    feat_send,
+    feat_sem,
+    bulk_send,
+    bulk_sem,
+    local_sem,
 ):
     x, k, y, g, b = (lax.axis_index(name) for name in AXES)
     slab = x * 2 + k
     line = g * 2 + b
+    me = x * 16 + k * 8 + y * 2 + b
+    row = slab * 32 + y * 8 + line
+
+    def group_peer(i):
+        t = lax.rem(me + i, 64)
+        return t, decode_group(t)
+
+    def row_peer(i):
+        return decode_all(lax.rem(row + 256 + i, 256))
 
     def slab_peer(i):
         t = lax.rem(slab + i, 8)
@@ -191,37 +219,170 @@
         t = lax.rem(g + i, 4)
         return t, {"g": t}
 
+    mesh_id = pl.DeviceIdType.MESH
     barrier = pltpu.get_barrier_semaphore()
-    for count, peer in ((8, slab_peer), (4, y_peer), (8, line_peer)):
-        for i in range(1, count):
+
+    def greet(i, _):
+        pl.semaphore_signal(barrier, inc=1, device_id=group_peer(i)[1], device_id_type=mesh_id)
+        return 0
+
+    for i in (-3, -2, -1, 1, 2, 3):
+        pl.semaphore_signal(barrier, inc=1, device_id=row_peer(i), device_id_type=mesh_id)
+    for i in range(1, 4):
+        for c in range(2):
             pl.semaphore_signal(
-                barrier, inc=1, device_id=peer(i)[1], device_id_type=pl.DeviceIdType.MESH
+                barrier,
+                inc=1,
+                device_id={"g": lax.rem(g + i, 4), "b": lax.rem(b + c, 2)},
+                device_id_type=mesh_id,
             )
-    pl.semaphore_wait(barrier, 17)
-
-    def send(source, target, slot, arrival, device):
+    lax.fori_loop(1, 64, greet, 0)
+    k_local = pltpu.make_async_copy(k_hbm.at[me], k_ref.at[me], local_sem.at[0])
+    m_local = pltpu.make_async_copy(m_hbm.at[me], m_ref.at[me], local_sem.at[1])
+    k_local.start()
+    m_local.start()
+    pl.semaphore_wait(barrier, 75)
+
+    def copy_to(source, target, departure, arrival, device):
         copy = pltpu.make_async_remote_copy(
             src_ref=source,
             dst_ref=target,
-            send_sem=send_sem.at[slot],
+            send_sem=departure,
             recv_sem=arrival,
             device_id=device,
-            device_id_type=pl.DeviceIdType.MESH,
+            device_id_type=mesh_id,
         )
         copy.start()
         return copy
 
+    def send(source, target, slot, arrival, device):
+        return copy_to(source, target, send_sem.at[slot], arrival, device)
+
+    def bulk(which, source, target):
+        def one(i, _):
+            t, device = group_peer(i)
+            copy_to(source.at[t], target.at[me], bulk_send.at[which], bulk_sem.at[which], device)
+            return 0
+
+        lax.fori_loop(1, 64, one, 0)
+
+    def bulk_wait(which, source, target):
+        pltpu.make_async_copy(
+            target.at[pl.ds(0, 63)], target.at[pl.ds(0, 63)], bulk_sem.at[which]
+        ).wait()
+        pltpu.make_async_copy(
+            source.at[pl.ds(0, 63)], source.at[pl.ds(0, 63)], bulk_send.at[which]
+        ).wait()
+
+    feat_copies = []
+    for n, i in enumerate((-1, 1, -2, 2, -3, 3)):
+        feat_copies.append(
+            copy_to(feat_ref, fbuf.at[3 - i], feat_send.at[n], feat_sem.at[n], row_peer(i))
+        )
+    bulk(0, k_hbm, k_ref)
     mask_copies = []
     for i in range(1, 8):
         mask_copies.append(
             send(mask_ref, mask_all.at[slab], i - 1, mask_sem.at[i - 1], slab_peer(i)[1])
         )
     mask_all[pl.ds(slab, 1)] = mask_ref[...][None]
+    bulk(1, m_hbm, m_ref)
+
+    fbuf[3] = feat_ref[...]
+    for copy in feat_copies:
+        copy.wait()
+    f_rows[14:16] = jnp.zeros((2, 8192), f32)
+    for r in range(7):
+        inside = jnp.logical_and(row + r >= 3, row + r < 259)
+        f_rows[2 * r : 2 * r + 2] = jnp.where(inside, fbuf[r].astype(f32), 0.0)
+    for dx in range(3):
+        shifted = column_shift(f_rows[...], dx - 1)
+        for dz in range(3):
+            tap = dz * 3 + dx
+            a1[16 * tap : 16 * tap + 16] = plane_shift(shifted, dz - 1).astype(bf16)
+
+    lane = lanes((1, 256))
+    hidden_row = row - 2 + jnp.minimum(lane // 32, 4)
+    keep1 = jnp.where(jnp.logical_and(hidden_row >= 0, hidden_row < 256), 1.0, 0.0)
+    lane = lanes((1, 128))
+    hidden_row = row - 1 + jnp.minimum(lane // 32, 2)
+    keep2 = jnp.where(jnp.logical_and(hidden_row >= 0, hidden_row < 256), 1.0, 0.0)
+    h1e[...] = jnp.zeros_like(h1e)
+
+    def layer_one(n, _):
+        first = pl.multiple_of(n * 512, 512)
+        block = lax.dot_general(
+            a1[:, pl.ds(first, 512)],
+            w1_ref[...],
+            (((0,), (0,)), ((), ())),
+            preferred_element_type=f32,
+        )
+        block = (jnp.maximum(block + b1_ref[...], 0.0) * keep1).astype(bf16)
+        h1m[pl.ds(pl.multiple_of(first + 128, 128), 512)] = block[:, :128]
+        for dz in range(3):
+            h1e[pl.ds(pl.multiple_of(first + 256 - 128 * dz, 128), 512), 32 * dz : 32 * dz + 32] = (
+                block[:, 128 + 32 * dz : 160 + 32 * dz]
+            )
+        return 0
+
+    lax.fori_loop(0, 16, layer_one, 0)
+    zero = jnp.zeros((64, 128), bf16)
+    h1m[0:64] = zero
+    h1m[64:128] = h1m[128 + 8064 : 128 + 8128]
+    h1m[128 + 8192 : 128 + 8256] = h1m[192:256]
+    h1m[128 + 8256 : 128 + 8320] = zero
+    h1e[128:192, 0:32] = jnp.zeros((64, 32), bf16)
+    h1e[192:256, 0:32] = h1e[128 + 8064 : 128 + 8128, 32:64]
+    return_rows = h1e[192:256, 32:64]
+    h1e[128 + 8064 : 128 + 8128, 64:96] = return_rows
+    h1e[128 + 8128 : 128 + 8192, 64:96] = jnp.zeros((64, 32), bf16)
+
+    def layer_two(n, _):
+        first = pl.multiple_of(n * 512, 512)
+        low = jnp.concatenate(
+            [
+                h1m[pl.ds(first, 512)],
+                h1m[pl.ds(pl.multiple_of(first + 128, 128), 512)],
+                h1m[pl.ds(pl.multiple_of(first + 256, 128), 512)],
+                h1e[pl.ds(pl.multiple_of(first + 128, 128), 512)],
+            ],
+            axis=1,
+        )
+        block = mm(low, w2_ref[...])
+        column = lax.rem(lax.broadcasted_iota(jnp.int32, (512, 128), 0), 64)
+        block = (
+            jnp.where(column != 0, pltpu.roll(block[:, :128], 1, 0), 0.0)
+            + block[:, 128:256]
+            + jnp.where(column != 63, pltpu.roll(block[:, 256:], 511, 0), 0.0)
+        )
+        block = (jnp.maximum(block + b2_ref[...], 0.0) * keep2).astype(bf16)
+        p3[:, pl.ds(first, 512)] = lax.dot_general(
+            w3_ref[...], block, (((1,), (1,)), ((), ())), preferred_element_type=f32
+        )
+        return 0
+
+    lax.fori_loop(0, 16, layer_two, 0)
+    total = jnp.zeros((8, 8192), f32)
+    for dx in range(3):
+        side = jnp.zeros((8, 8192), f32)
+        for dz in range(3):
+            tap = dz * 3 + dx
+            side = side + plane_shift(p3[8 * tap : 8 * tap + 8], dz - 1)
+        total = total + column_shift(side, dx - 1)
+    total = total[0:2] + (prior_ref[...] + b3_ref[...])
+    for i in range(64):
+        for c in range(2):
+            dplanes[c, i : i + 1] = total[c : c + 1, 128 * i : 128 * i + 128]
+    for c in range(2):
+        turned = jnp.transpose(dplanes[c])
+        dsrc[:, c] = jnp.concatenate([turned[:64], turned[64:]], axis=1)
+    bulk(2, dsrc, dbuf)
+    dbuf[pl.ds(me, 1)] = dsrc[pl.ds(me, 1)]
 
     acc[...] = jnp.zeros_like(acc)
 
     def maps_of(j):
-        return s_ref[j, 0].astype(f32), s_ref[j, 1].astype(f32)
+        return s_ref[j, 0], s_ref[j, 1]
 
     def add_image(image, pair):
         for n in range(2):
@@ -231,15 +392,29 @@
             acc[0] += real * a_real + imag * a_imag
             acc[1] += real * a_imag - imag * a_real
 
+    k_local.wait()
+    m_local.wait()
+    bulk_wait(0, k_hbm, k_ref)
+    bulk_wait(1, m_hbm, m_ref)
+
     def adjoint_pair(pair, _):
         planes = []
         for n in range(2):
             j = 2 * pair + n
             planes.append(
                 jnp.concatenate(
-                    [k_ref[:, j, 0].reshape(128, 256), k_ref[:, j, 1].reshape(128, 256)], axis=1
+                    [
+                        jnp.concatenate([k_ref[8 * s + j, c] for s in range(8)], axis=0)
+                        for c in range(2)
+                    ],
+                    axis=1,
                 )
             )
+            for c in range(2):
+                for h in range(4):
+                    for s in range(8):
+                        first = h * 64 + s * 8
+                        s_ref[j, c, first : first + 8] = m_ref[8 * s + j, c, h].astype(f32)
         spectrum = jnp.concatenate(planes, axis=0)
         dims = (((1,), (1,)), ((), ()))
         rows = lax.dot_general(
@@ -291,7 +466,9 @@
             )
         return copies
 
-    right = reduce_scatter(0)() + penalty * den_ref[...]
+    right = reduce_scatter(0)()
+    bulk_wait(2, dsrc, dbuf)
+    right = right + penalty * jnp.stack([dbuf[:, 0], dbuf[:, 1]])
     gathers = gather(0, right)
     for copy in mask_copies:
         copy.wait_recv()
@@ -380,21 +557,83 @@
     growth = fresh / rr
     step_size = fresh / (energy + penalty * fresh - growth * fresh / alpha)
     q = finish() + penalty * residual + growth * image
-    sol_ref[...] = alpha * right + step_size * (residual + growth * right)
-    res_ref[...] = residual - step_size * q
-
-
-def cg(den, spectrum, maps, mask):
+    answer = alpha * right + step_size * (residual + growth * right)
+    rest = residual - step_size * q
+    for c in range(2):
+        osrc[:, c] = answer[c]
+        osrc[:, 2 + c] = rest[c]
+    bulk(3, osrc, obuf)
+    obuf[pl.ds(me, 1)] = osrc[pl.ds(me, 1)]
+    bulk_wait(3, osrc, obuf)
+    sol_ref[...] = jnp.transpose(jnp.concatenate([obuf[:, 0], obuf[:, 1]], axis=0))
+    res_ref[...] = jnp.transpose(jnp.concatenate([obuf[:, 2], obuf[:, 3]], axis=0))
+
+
+def body(
+    prior_image,
+    coil_maps,
+    kspace,
+    sampling,
+    weight_first,
+    bias_first,
+    weight_middle,
+    bias_middle,
+    weight_last,
+    bias_last,
+):
+    mask = sampling.astype(bf16)
+    measured = kspace[0] * mask[:, :, None]
+    spectrum = measured.reshape(16, 256, 2, 64).transpose(3, 2, 0, 1)
+    maps = coil_maps[0].reshape(4, 4, 2, 128, 2, 64).transpose(5, 4, 1, 0, 2, 3)
+    maps = maps.reshape(64, 2, 4, 8, 128)
+    prior = prior_image.reshape(2, 64, 2, 64).transpose(2, 1, 0, 3).reshape(2, 8192)
+    features = prior.astype(bf16)
+
+    first = weight_first.transpose(1, 2, 0, 4, 3).reshape(9, 6, 32)
+    pieces = [jnp.pad(first, ((0, 0), (2 * r, 10 - 2 * r), (0, 0))) for r in (0, 1, 2, 3, 4, 4, 4)]
+    w1 = jnp.pad(jnp.concatenate(pieces, axis=2), ((0, 0), (0, 0), (0, 32))).reshape(144, 256)
+    middle = weight_middle.transpose(1, 0, 4, 2, 3).reshape(3, 96, 3, 32)
+    pieces = [jnp.pad(middle, ((0, 0), (32 * r, 64 - 32 * r), (0, 0), (0, 0))) for r in range(3)]
+    middle = jnp.concatenate(pieces + [jnp.zeros_like(pieces[0])], axis=3).reshape(3, 160, 384)
+    w2 = jnp.concatenate(
+        [
+            middle[:, :128].reshape(384, 384),
+            middle[:, 128:].reshape(96, 384),
+            jnp.zeros((32, 384), bf16),
+        ],
+        axis=0,
+    )
+    w3 = weight_last.transpose(1, 2, 3, 0, 4).reshape(9, 2, 96)
+    w3 = jnp.pad(w3, ((0, 0), (0, 6), (0, 32))).reshape(72, 128)
+    b1 = jnp.tile(bias_first, 8)[None]
+    b2 = jnp.tile(bias_middle, 4)[None]
+    b3 = bias_last[:, None]
+
     forward, backward, z_forward, z_backward = tables()
     vmem = pl.BlockSpec(memory_space=pltpu.VMEM)
-    out = jax.ShapeDtypeStruct((2, 64, 128), f32)
+    hbm = pl.BlockSpec(memory_space=pl.ANY)
+    out = jax.ShapeDtypeStruct((128, 128), f32)
     dma = pltpu.SemaphoreType.DMA
-    return pl.pallas_call(
-        cg_kernel,
+    sol, res = pl.pallas_call(
+        step_kernel,
         out_shape=(out, out),
-        in_specs=[vmem] * 8,
+        in_specs=[vmem] * 2 + [hbm] * 2 + [vmem] * 11,
         out_specs=(vmem, vmem),
         scratch_shapes=[
+            pltpu.VMEM((64, 2, 16, 256), bf16),
+            pltpu.VMEM((64, 2, 4, 8, 128), bf16),
+            pltpu.VMEM((8, 2, 256, 128), f32),
+            pltpu.VMEM((7, 2, 8192), bf16),
+            pltpu.VMEM((16, 8192), f32),
+            pltpu.VMEM((144, 8192), bf16),
+            pltpu.VMEM((8448, 128), bf16),
+            pltpu.VMEM((8448, 128), bf16),
+            pltpu.VMEM((72, 8192), f32),
+            pltpu.VMEM((2, 64, 128), f32),
+            pltpu.VMEM((64, 2, 128), f32),
+            pltpu.VMEM((64, 2, 128), f32),
+            pltpu.VMEM((64, 4, 128), f32),
+            pltpu.VMEM((64, 4, 128), f32),
             pltpu.VMEM((2, 256, 128), f32),
             pltpu.VMEM((8, 16, 256), bf16),
             pltpu.VMEM((256, 128), f32),
@@ -412,69 +651,33 @@
             dma((2, 7)),
             dma((2, 3)),
             dma((2, 7)),
+            dma((6,)),
+            dma((6,)),
+            dma((4,)),
+            dma((4,)),
+            dma((2,)),
         ],
         compiler_params=pltpu.CompilerParams(
             collective_id=0, has_side_effects=True, vmem_limit_bytes=60 * 1024 * 1024
         ),
     )(
-        den,
+        features,
+        prior,
         spectrum,
         maps,
         mask,
+        w1,
+        w2,
+        w3,
+        b1,
+        b2,
+        b3,
         jnp.asarray(forward),
         jnp.asarray(backward),
         jnp.asarray(z_forward),
         jnp.asarray(z_backward),
     )
-
-
-def body(
-    prior_image,
-    coil_maps,
-    kspace,
-    sampling,
-    weight_first,
-    bias_first,
-    weight_middle,
-    bias_middle,
-    weight_last,
-    bias_last,
-):
-    readout = prior_image.shape[2] // 2
-    own_rows = prior_image.shape[0]
-    planes = prior_image.shape[1]
-
-    def exchange(value):
-        return lax.all_to_all(value, GROUP, split_axis=0, concat_axis=0, tiled=True)
-
-    mask = sampling.astype(bf16)
-    measured = kspace[0] * mask[:, :, None]
-    spectrum = exchange(measured.reshape(16, 256, 2, 64).transpose(3, 2, 0, 1))
-    spectrum = spectrum.reshape(8, 8, 2, 16, 256)
-    maps = coil_maps[0].reshape(4, 4, 2, 128, 2, 64).transpose(5, 4, 1, 0, 2, 3)
-    maps = exchange(maps.reshape(64, 2, 4, 8, 128))
-    maps = maps.reshape(8, 8, 2, 4, 8, 128).transpose(1, 2, 3, 0, 4, 5).reshape(8, 2, 256, 128)
-
-    features = (
-        jnp.stack([prior_image[..., :readout], prior_image[..., readout:]], axis=1)
-        .reshape(own_rows, 2, planes * readout)
-        .astype(jnp.bfloat16)
-    )
-    hidden = jax.nn.relu(convolve_layer(features, weight_first, bias_first, readout)).astype(
-        jnp.bfloat16
-    )
-    hidden = jax.nn.relu(convolve_layer(hidden, weight_middle, bias_middle, readout)).astype(
-        jnp.bfloat16
-    )
-    output = convolve_layer(hidden, weight_last, bias_last, readout).reshape(
-        own_rows, 2, planes, readout
-    )
-    denoised = prior_image + jnp.concatenate([output[:, 0], output[:, 1]], axis=-1)
-    den = exchange(denoised[0].reshape(128, 2, 64).transpose(2, 1, 0)).transpose(1, 0, 2)
-    sol, res = cg(den, spectrum, maps, mask)
-    both = exchange(jnp.stack([sol, res]).transpose(2, 0, 1, 3))
-    both = both.transpose(1, 3, 2, 0).reshape(2, 1, 128, 128)
-    return both[0], both[1]
+    return sol[None], res[None]
 
 
 def solution(mesh):

time: 242 us -> 146 us (0.60)
  waiting for transfers between devices: 54 us -> 0 us
  starting transfers between devices: 50.8 us -> 0 us
  Pallas kernels: 84.8 us -> 129 us
  blocking collectives: 14.7 us -> 0 us
  local copies, waits for them, and re-layouts: 22.1 us -> 12.8 us
  matrix products: 9.25 us -> 0 us
    pallas_call x1, Pallas kernels: 84.8 us -> 129 us  [body(): pl.pallas_call(step_kernel, out_shape=(out, out), in_specs=[vmem] * 2 + [...]
    all_to_all x3 -> x0, waiting for transfers between devices: 37.2 us -> none  [exchange(): return lax.all_to_all(value, GROUP, split_axis=0, concat_axis=0, tiled=True)]
    ppermute x6 -> x0, starting transfers between devices: 31.7 us -> none  [the longest x3 23.5 us: with_halo(): high = lax.ppermute(initial, ALL, [(b, a) for a, b in up])]
    all_to_all x3 -> x0, starting transfers between devices: 19 us -> none  [exchange(): return lax.all_to_all(value, GROUP, split_axis=0, concat_axis=0, tiled=True)]
    ppermute x6 -> x0, waiting for transfers between devices: 16.8 us -> none  [the longest x3 15.9 us: with_halo(): low = lax.ppermute(last, ALL, up)]
    all_to_all x1 -> x0, blocking collectives: 14.7 us -> none  [exchange(): return lax.all_to_all(value, GROUP, split_axis=0, concat_axis=0, tiled=True)]
    dot_general x27 -> x0, matrix products: 9.25 us -> none  [convolve_layer(): jnp.einsum('oc,ycn->yon', kernel, stacked, preferred_element_type=jnp.flo...]
    slice x10 -> x2, local copies, waits for them, and re-layouts: 7.19 us -> 0.11 us  [the longest x1 0.05 us: body(): middle[:, 128:].reshape(96, 384)]
  transfers between devices with their start and end apart: 9 -> 0, of which waited for: 6 -> 0; matrix products, arithmetic and copies ran while one was open for 4% -> 0% of each run, Pallas kernels for 0% -> 0%
where the time goes in v2:
time: 146 us
  Pallas kernels  129 us (88%)
  local copies, waits for them, and re-layouts  12.8 us (9%)
  other arithmetic  3.27 us (2%)
    pallas_call x1, Pallas kernels, body(): pl.pallas_call(step_kernel, out_shape=(out, out), in_specs=[vmem] * 2 + [...  129 us
    unnamed x26, local copies, waits for them, and re-layouts  5.53 us

profile of v2, /device:TPU:1, one launch (start us, length us, event | category | flops | bytes accessed | tf_op | source)
XLA Modules:
  0.0 146.1 jit_solution(12843356821492442484)
XLA Ops:
  0.6 1.0 reshape.42
  1.6 0.1 copy.36
  1.7 0.2 reshape.43.prior_ref
  1.9 0.6 convert_element_type.28.feat_ref
  2.5 1.5 %copy.20 = bf16[1,16,256,128]{2,3,1,0:T(8,128)(2,1)S(1)} copy(bf16[1,16,256,128]{3,2,1,0:T(8,128)(2,1)} %param.16) | data formatting | bytes 2097152 | tf_op args[2]
  4.1 0.0 copy-start
  4.1 1.6 %fusion.5.k_hbm = bf16[64,2,16,256]{3,2,1,0:T(8,128)(2,1)} fusion(bf16[16,256,2,64]{1,3,2,0:T(8,128)(2,1)S(1)} %bitcast.25, bf16[16,256]{1,0:T(8,128)(2,1)S(1)} %convert_element_type.29.mask_ref), kind=kLoop, calls=%fused_computation.11 | loop fusion | flops 524288 | bytes 2105344 | tf_op jit(solution)/shard_map/transpose | solution.py:586
  5.7 0.7 copy.22
  6.3 0.0 copy-start.5
  6.3 2.1 %copy.23 = bf16[64,2,4,4,2,128]{5,4,3,2,1,0:T(2,128)(2,1)} copy(bf16[64,2,4,4,2,128]{5,0,1,4,2,3:T(8,128)(2,1)S(1)} %bitcast.26) | data formatting | bytes 2097152 | tf_op jit(solution)/shard_map/transpose | solution.py:587
  8.5 0.1 concatenate.9
  8.7 0.6 pad.47
  9.3 0.2 copy.25
  9.5 0.2 reshape.47
  9.7 0.1 pad.58.clone
  9.7 0.2 fusion.7
  9.9 0.1 slice.9
  10.0 0.2 copy.31
  10.2 0.0 copy-start.8
  10.2 0.0 copy-start.9
  10.2 0.1 slice.8
  10.3 0.2 copy.30
  10.5 0.1 pad.54.clone
  10.5 0.9 maximum_maximum_fusion.w2_ref
  11.5 0.1 reshape.51
  11.6 0.6 pad_bitcast_fusion.w3_ref
  12.2 0.6 broadcast_in_dim_tile.6.b1_ref
  12.8 0.6 broadcast_in_dim_tile.7.b2_ref
  13.3 0.6 copy.28.b3_ref
  14.0 129.2 %shard_map.149 = (f32[128,128]{1,0:T(8,128)}, f32[128,128]{1,0:T(8,128)}) custom-call(bf16[2,8192]{1,0:T(2,128)(2,1)} %convert_element_type.28.feat_ref, f32[2,8192]{1,0:T(2,128)} %copy-done.1, bf16[64,2,16,256]{3,2,1,0:T(8,128)(2,1)} %fusion.5.k_hbm, bf16[64,2,4,8,128]{4,3,2,1,0:T(8,128)(2,1)} %bitcast.24, bf16[16,256]{1,0:T(8,128)(2,1)} %copy-done.3, ...), custom_call_target="tpu_custom_call" | custom-call | tf_op jit(solution)/shard_map/pallas_call | solution.py:617
  143.2 1.5 %copy.39 = f32[1,128,128]{2,1,0:T(8,128)} copy(f32[1,128,128]{2,1,0:T(8,128)} %bitcast.35) | data formatting | bytes 131072
  144.7 1.5 %copy.40 = f32[1,128,128]{2,1,0:T(8,128)} copy(f32[1,128,128]{2,1,0:T(8,128)} %bitcast.34) | data formatting | bytes 131072
  (24 shorter events, 0.1 us)
Async XLA Ops:
  1.9 2.2 %copy-start.1 = (f32[2,8192]{1,0:T(2,128)}, f32[2,8192]{1,0:T(2,128)S(1)}, u32[]{:S(2)}) copy-start(f32[2,8192]{1,0:T(2,128)S(1)} %reshape.43.prior_ref) | copy-start | bytes 196612
  2.5 1.5 %copy-start.4 = (s32[16,256]{1,0:T(8,128)S(1)}, s32[16,256]{1,0:T(8,128)}, u32[]{:S(2)}) copy-start(s32[16,256]{1,0:T(8,128)} %param.17) | copy-start | bytes 49156
  4.1 1.6 %copy-start.3 = (bf16[16,256]{1,0:T(8,128)(2,1)}, bf16[16,256]{1,0:T(8,128)(2,1)S(1)}, u32[]{:S(2)}) copy-start(bf16[16,256]{1,0:T(8,128)(2,1)S(1)} %convert_element_type.29.mask_ref) | copy-start | bytes 24580
  4.1 1.6 %copy-start = (bf16[1,32,128,128]{3,2,1,0:T(8,128)(2,1)S(1)}, bf16[1,32,128,128]{3,2,1,0:T(8,128)(2,1)}, u32[]{:S(2)}) copy-start(bf16[1,32,128,128]{3,2,1,0:T(8,128)(2,1)} %param.15) | copy-start | bytes 3145732
  6.3 2.1 %copy-start.5 = (bf16[3,3,3,32,2]{3,4,2,1,0:T(2,128)(2,1)S(1)}, bf16[3,3,3,32,2]{3,4,2,1,0:T(2,128)(2,1)}, u32[]{:S(2)}) copy-start(bf16[3,3,3,32,2]{3,4,2,1,0:T(2,128)(2,1)} %param.18) | copy-start | bytes 10372
  6.3 3.0 %copy-start.2 = (bf16[3,3,3,32,32]{4,3,2,1,0:T(8,128)(2,1)S(1)}, bf16[3,3,3,32,32]{4,3,2,1,0:T(8,128)(2,1)}, u32[]{:S(2)}) copy-start(bf16[3,3,3,32,32]{4,3,2,1,0:T(8,128)(2,1)} %param.20) | copy-start | bytes 165892
  10.1 1.3 copy-start.6
  10.2 2.0 %copy-start.7 = (f32[32]{0:T(128)S(1)}, f32[32]{0:T(128)}, u32[]{:S(2)}) copy-start(f32[32]{0:T(128)} %param.19) | copy-start | bytes 388
  10.2 2.6 %copy-start.8 = (f32[32]{0:T(128)S(1)}, f32[32]{0:T(128)}, u32[]{:S(2)}) copy-start(f32[32]{0:T(128)} %param.21) | copy-start | bytes 388
  10.2 3.2 %copy-start.9 = (f32[2]{0:T(128)S(1)}, f32[2]{0:T(128)}, u32[]{:S(2)}) copy-start(f32[2]{0:T(128)} %param.23) | copy-start | bytes 28

commit v3 on v2

v3 whole, which is shorter than its diff:
```python
import functools

import jax
import jax.numpy as jnp
import numpy as np
from jax import lax
from jax.experimental import pallas as pl
from jax.experimental.pallas import tpu as pltpu
from jax.sharding import Mesh
from jax.sharding import PartitionSpec as P

AXES = ("x", "k", "y", "g", "b")
SIZES = (4, 2, 4, 4, 2)
GROUP = ("x", "k", "y", "b")
ALL = ("x", "k", "y", "g", "b")

penalty = 0.5
f32 = jnp.float32
bf16 = jnp.bfloat16


def split_table(table):
    table = table.astype(np.float32)
    high = table.astype(jnp.bfloat16)
    low = (table - high.astype(np.float32)).astype(jnp.bfloat16)
    return np.stack([high, low])


def row_order():
    order = np.zeros(256, np.int64)
    for g in range(4):
        for s in range(8):
            for y in range(4):
                for b in range(2):
                    order[g * 64 + s * 8 + y * 2 + b] = s * 32 + y * 8 + 2 * g + b
    return order


def tables():
    rows = row_order().reshape(4, 2, 32)[:, 0].reshape(128)
    forward, backward = [], []
    for parity in range(2):
        angle = 2 * np.pi * (np.outer(2 * np.arange(128) + parity, rows) % 256) / 256
        c, s = np.cos(angle) / 16.0, np.sin(angle) / 16.0
        forward.append(split_table(np.block([[c, s], [-s, c]])))
        backward.append(split_table(np.block([[c.T, -s.T], [s.T, c.T]])))
    angle = 2 * np.pi * (np.outer(np.arange(128), np.arange(128)) % 128) / 128
    c, s = np.cos(angle) / np.sqrt(128.0), np.sin(angle) / np.sqrt(128.0)
    z_forward = split_table(np.block([[c, -s], [s, c]]))
    z_backward = split_table(np.block([[c, s], [-s, c]]))
    return np.stack(forward), np.stack(backward), z_forward, z_backward


def halves(value):
    high = value.astype(bf16)
    low = (value - high.astype(f32)).astype(bf16)
    return high, low


def mm(a, b):
    return jnp.dot(a, b, preferred_element_type=f32)


def table_right(value, table):
    high, low = halves(value)
    return mm(high, table[0]) + (mm(high, table[1]) + mm(low, table[0]))


def table_left(table, value):
    high, low = halves(value)
    return mm(table[0], high) + (mm(table[1], high) + mm(table[0], low))


def split_rows(value):
    sums, differences = [], []
    for n in range(2):
        low = jnp.concatenate([value[256 * n + 64 * h :][:32] for h in range(4)], axis=0)
        high = jnp.concatenate([value[256 * n + 64 * h + 32 :][:32] for h in range(4)], axis=0)
        for out, part in ((sums, low + high), (differences, low - high)):
            out.append(jnp.concatenate([part[:, :128], part[:, 128:]], axis=0))
    return jnp.concatenate(sums, axis=1), jnp.concatenate(differences, axis=1)


def join_rows(even, odd):
    low, high = even + odd, even - odd
    pieces = []
    for n in range(2):
        first = slice(128 * n, 128 * n + 128)
        parts = [jnp.concatenate([p[:128, first], p[128:, first]], axis=1) for p in (low, high)]
        for h in range(4):
            for part in parts:
                pieces.append(part[32 * h : 32 * h + 32])
    return jnp.concatenate(pieces, axis=0)


def coded(value):
    peak = jnp.maximum(jnp.max(jnp.abs(value), axis=1, keepdims=True), 1e-30)
    code = jnp.round(value * (32767.0 / peak)).astype(jnp.int32).astype(jnp.int16)
    return code, peak[:, 0]


def decoded(code, peak):
    return code.astype(jnp.int32).astype(f32) * (peak * (1.0 / 32767.0))[:, None]


def folded(value):
    return value.reshape(-1, 8, 128).sum(axis=0)


def decode_all(i):
    return {
        "x": i // 64,
        "k": lax.rem(i // 32, 2),
        "y": lax.rem(i // 8, 4),
        "g": lax.rem(i // 2, 4),
        "b": lax.rem(i, 2),
    }


def lanes(shape):
    return lax.broadcasted_iota(jnp.int32, shape, len(shape) - 1)


def plane_shift(value, dz):
    if dz == 0:
        return value
    if dz < 0:
        edge = pltpu.roll(value[:, -128:], 64, 1)
        edge = jnp.where(lanes(edge.shape) >= 64, edge, 0.0)
        return jnp.concatenate([edge, value[:, :-128]], axis=1)
    edge = pltpu.roll(value[:, :128], 64, 1)
    edge = jnp.where(lanes(edge.shape) < 64, edge, 0.0)
    return jnp.concatenate([value[:, 128:], edge], axis=1)


def column_shift(value, dx):
    if dx == 0:
        return value
    width = value.shape[1]
    column = lax.rem(lanes(value.shape), 64)
    if dx < 0:
        return jnp.where(column != 0, pltpu.roll(value, 1, 1), 0.0)
    return jnp.where(column != 63, pltpu.roll(value, width - 1, 1), 0.0)


def step_kernel(
    prior_ref,
    k_hbm,
    m_hbm,
    mask_ref,
    w1_ref,
    w2_ref,
    w3_ref,
    b1_ref,
    b2_ref,
    b3_ref,
    fy_ref,
    gy_ref,
    fz_ref,
    gz_ref,
    out_ref,
    k_ref,
    m_ref,
    s_ref,
    feat,
    fbuf,
    f_rows,
    a1,
    h1m,
    h1e,
    p3,
    dplanes,
    dsrc,
    dbuf,
    osrc,
    obuf,
    acc,
    mask_all,
    mask_t,
    spectra,
    out_code,
    out_peak,
    part_code,
    part_peak,
    own_code,
    own_peak,
    full_code,
    full_peak,
    full,
    stat_a,
    stat_b,
    stat_c,
    stat_own,
    send_sem,
    part_sem,
    full_sem,
    mask_sem,
    stat_sem_a,
    stat_sem_b,
    stat_sem_c,
    feat_send,
    feat_sem,
    bulk_send,
    bulk_sem,
    local_sem,
):
    x, k, y, g, b = (lax.axis_index(name) for name in AXES)
    slab = x * 2 + k
    line = g * 2 + b
    me = x * 16 + k * 8 + y * 2 + b
    row = slab * 32 + y * 8 + line

    xs = [lax.rem(x + i, 4) for i in range(4)]
    ks = [k, 1 - k]
    ys = [lax.rem(y + i, 4) for i in range(4)]
    bs = [b, 1 - b]
    group = []
    for n in range(64):
        i, j = n % 4, n // 4 % 4
        offset = (i, (n // 16 + j) % 2, (i + j) % 4, (n // 32 + i) % 2)
        if any(offset):
            there = xs[offset[0]], ks[offset[1]], ys[offset[2]], bs[offset[3]]
            index = there[0] * 16 + there[1] * 8 + there[2] * 2 + there[3]
            group.append((index, dict(zip(GROUP, there))))

    def row_peer(i):
        return decode_all(lax.rem(row + 256 + i, 256))

    def slab_peer(i):
        t = lax.rem(slab + i, 8)
        return t, {"x": t // 2, "k": lax.rem(t, 2)}

    def y_peer(i):
        t = lax.rem(y + i, 4)
        return t, {"y": t}

    def line_peer(i):
        t = lax.rem(line + i, 8)
        return t, {"g": t // 2, "b": lax.rem(t, 2)}

    def g_peer(i):
        t = lax.rem(g + i, 4)
        return t, {"g": t}

    mesh_id = pl.DeviceIdType.MESH
    barrier = pltpu.get_barrier_semaphore()

    for _, device in group:
        pl.semaphore_signal(barrier, inc=1, device_id=device, device_id_type=mesh_id)
    for i in (-3, -2, -1, 1, 2, 3):
        pl.semaphore_signal(barrier, inc=1, device_id=row_peer(i), device_id_type=mesh_id)
    for i in range(1, 4):
        for c in range(2):
            pl.semaphore_signal(
                barrier,
                inc=1,
                device_id={"g": lax.rem(g + i, 4), "b": lax.rem(b + c, 2)},
                device_id_type=mesh_id,
            )
    feat[...] = prior_ref[...].astype(bf16)
    k_local = pltpu.make_async_copy(k_hbm.at[me], k_ref.at[me], local_sem.at[0])
    m_local = pltpu.make_async_copy(m_hbm.at[me], m_ref.at[me], local_sem.at[1])
    k_local.start()
    m_local.start()
    pl.semaphore_wait(barrier, 75)

    def copy_to(source, target, departure, arrival, device):
        copy = pltpu.make_async_remote_copy(
            src_ref=source,
            dst_ref=target,
            send_sem=departure,
            recv_sem=arrival,
            device_id=device,
            device_id_type=mesh_id,
        )
        copy.start()
        return copy

    def send(source, target, slot, arrival, device):
        return copy_to(source, target, send_sem.at[slot], arrival, device)

    def bulk(*jobs):
        for t, device in group:
            for which, source, target in jobs:
                copy_to(
                    source.at[t], target.at[me], bulk_send.at[which], bulk_sem.at[which], device
                )

    def bulk_wait(which, source, target):
        pltpu.make_async_copy(
            target.at[pl.ds(0, 63)], target.at[pl.ds(0, 63)], bulk_sem.at[which]
        ).wait()
        pltpu.make_async_copy(
            source.at[pl.ds(0, 63)], source.at[pl.ds(0, 63)], bulk_send.at[which]
        ).wait()

    feat_copies = []
    for n, i in enumerate((-1, 1, -2, 2, -3, 3)):
        feat_copies.append(
            copy_to(feat, fbuf.at[3 - i], feat_send.at[n], feat_sem.at[n], row_peer(i))
        )
    mask_copies = []
    for i in range(1, 8):
        mask_copies.append(
            send(mask_ref, mask_all.at[slab], i - 1, mask_sem.at[i - 1], slab_peer(i)[1])
        )
    mask_all[pl.ds(slab, 1)] = mask_ref[...][None]
    bulk((0, k_hbm, k_ref), (1, m_hbm, m_ref))

    fbuf[3] = feat[...]
    for copy in feat_copies:
        copy.wait()
    f_rows[14:16] = jnp.zeros((2, 8192), f32)
    for r in range(7):
        inside = jnp.logical_and(row + r >= 3, row + r < 259)
        f_rows[2 * r : 2 * r + 2] = jnp.where(inside, fbuf[r].astype(f32), 0.0)
    for dx in range(3):
        shifted = column_shift(f_rows[...], dx - 1)
        for dz in range(3):
            tap = dz * 3 + dx
            a1[16 * tap : 16 * tap + 16] = plane_shift(shifted, dz - 1).astype(bf16)

    bias_one = jnp.concatenate([b1_ref[...]] * 8, axis=1)
    bias_two = jnp.concatenate([b2_ref[...]] * 4, axis=1)
    lane = lanes((1, 256))
    hidden_row = row - 2 + jnp.minimum(lane // 32, 4)
    keep1 = jnp.where(jnp.logical_and(hidden_row >= 0, hidden_row < 256), 1.0, 0.0)
    lane = lanes((1, 128))
    hidden_row = row - 1 + jnp.minimum(lane // 32, 2)
    keep2 = jnp.where(jnp.logical_and(hidden_row >= 0, hidden_row < 256), 1.0, 0.0)
    h1e[...] = jnp.zeros_like(h1e)

    def layer_one(n, _):
        first = pl.multiple_of(n * 512, 512)
        block = lax.dot_general(
            a1[:, pl.ds(first, 512)],
            w1_ref[...],
            (((0,), (0,)), ((), ())),
            preferred_element_type=f32,
        )
        block = (jnp.maximum(block + bias_one, 0.0) * keep1).astype(bf16)
        h1m[pl.ds(pl.multiple_of(first + 128, 128), 512)] = block[:, :128]
        for dz in range(3):
            h1e[pl.ds(pl.multiple_of(first + 256 - 128 * dz, 128), 512), 32 * dz : 32 * dz + 32] = (
                block[:, 128 + 32 * dz : 160 + 32 * dz]
            )
        return 0

    lax.fori_loop(0, 16, layer_one, 0)
    zero = jnp.zeros((64, 128), bf16)
    h1m[0:64] = zero
    h1m[64:128] = h1m[128 + 8064 : 128 + 8128]
    h1m[128 + 8192 : 128 + 8256] = h1m[192:256]
    h1m[128 + 8256 : 128 + 8320] = zero
    h1e[128:192, 0:32] = jnp.zeros((64, 32), bf16)
    h1e[192:256, 0:32] = h1e[128 + 8064 : 128 + 8128, 32:64]
    return_rows = h1e[192:256, 32:64]
    h1e[128 + 8064 : 128 + 8128, 64:96] = return_rows
    h1e[128 + 8128 : 128 + 8192, 64:96] = jnp.zeros((64, 32), bf16)

    def layer_two(n, _):
        first = pl.multiple_of(n * 512, 512)
        low = jnp.concatenate(
            [
                h1m[pl.ds(first, 512)],
                h1m[pl.ds(pl.multiple_of(first + 128, 128), 512)],
                h1m[pl.ds(pl.multiple_of(first + 256, 128), 512)],
                h1e[pl.ds(pl.multiple_of(first + 128, 128), 512)],
            ],
            axis=1,
        )
        block = mm(low, w2_ref[...])
        column = lax.rem(lax.broadcasted_iota(jnp.int32, (512, 128), 0), 64)
        block = (
            jnp.where(column != 0, pltpu.roll(block[:, :128], 1, 0), 0.0)
            + block[:, 128:256]
            + jnp.where(column != 63, pltpu.roll(block[:, 256:], 511, 0), 0.0)
        )
        block = (jnp.maximum(block + bias_two, 0.0) * keep2).astype(bf16)
        p3[:, pl.ds(first, 512)] = lax.dot_general(
            w3_ref[...], block, (((1,), (1,)), ((), ())), preferred_element_type=f32
        )
        return 0

    lax.fori_loop(0, 16, layer_two, 0)
    total = jnp.zeros((8, 8192), f32)
    for dx in range(3):
        side = jnp.zeros((8, 8192), f32)
        for dz in range(3):
            tap = dz * 3 + dx
            side = side + plane_shift(p3[8 * tap : 8 * tap + 8], dz - 1)
        total = total + column_shift(side, dx - 1)
    channel = lax.broadcasted_iota(jnp.int32, (2, 1), 0)
    total = total[0:2] + (prior_ref[...] + jnp.where(channel == 0, b3_ref[0], b3_ref[1]))
    for i in range(64):
        for c in range(2):
            dplanes[c, i : i + 1] = total[c : c + 1, 128 * i : 128 * i + 128]
    for c in range(2):
        turned = jnp.transpose(dplanes[c])
        dsrc[:, c] = jnp.concatenate([turned[:64], turned[64:]], axis=1)
    bulk((2, dsrc, dbuf))
    dbuf[pl.ds(me, 1)] = dsrc[pl.ds(me, 1)]

    acc[...] = jnp.zeros_like(acc)

    def maps_of(j):
        return s_ref[j, 0], s_ref[j, 1]

    def add_image(image, pair):
        for n in range(2):
            real, imag = maps_of(2 * pair + n)
            a_real = image[256 * n : 256 * n + 256, :128]
            a_imag = image[256 * n : 256 * n + 256, 128:]
            acc[0] += real * a_real + imag * a_imag
            acc[1] += real * a_imag - imag * a_real

    k_local.wait()
    m_local.wait()
    bulk_wait(0, k_hbm, k_ref)
    bulk_wait(1, m_hbm, m_ref)

    for copy in mask_copies:
        copy.wait()
    half = lax.broadcasted_iota(jnp.int32, (256, 256), 0)
    eye = (half == lax.broadcasted_iota(jnp.int32, (256, 256), 1)).astype(bf16)
    mask_rows = mask_all[...].reshape(128, 256)
    by_line = (((1,), (1,)), ((), ()))
    mask_t[...] = lax.dot_general(eye, mask_rows, by_line, preferred_element_type=f32)

    def adjoint_pair(pair, _):
        sides = []
        for p in range(2):
            cells = slice(128 * p, 128 * p + 128)
            planes = []
            for n in range(2):
                for c in range(2):
                    plane = jnp.concatenate(
                        [k_ref[8 * s + 2 * pair + n, c][:, cells] for s in range(8)], axis=0
                    )
                    planes.append(plane * mask_rows[:, cells])
            spectrum = jnp.concatenate(
                [
                    jnp.concatenate(planes[0:2], axis=1),
                    jnp.concatenate(planes[2:4], axis=1),
                ],
                axis=0,
            )
            sides.append(
                lax.dot_general(gy_ref[p, 0], spectrum, by_line, preferred_element_type=f32)
                + lax.dot_general(gy_ref[p, 1], spectrum, by_line, preferred_element_type=f32)
            )
        for n in range(2):
            j = 2 * pair + n
            for c in range(2):
                for h in range(4):
                    for s in range(8):
                        first = h * 64 + s * 8
                        s_ref[j, c, first : first + 8] = m_ref[8 * s + j, c, h].astype(f32)
        add_image(table_right(join_rows(*sides), gz_ref), pair)
        return 0

    lax.fori_loop(0, 4, adjoint_pair, 0)

    mine = pl.ds(pl.multiple_of(g * 64, 64), 64)

    def reduce_scatter(step):
        copies = []
        for i in range(1, 4):
            t, device = g_peer(i)
            code, peak = coded(acc[:, pl.ds(pl.multiple_of(t * 64, 64), 64)])
            out_code[step, i - 1] = code
            out_peak[step, i - 1] = peak
            for n, (source, target) in enumerate(((out_code, part_code), (out_peak, part_peak))):
                copies.append(
                    send(
                        source.at[step, i - 1],
                        target.at[step, i - 1],
                        13 + 2 * i + n,
                        part_sem.at[step, i - 1, n],
                        device,
                    )
                )

        def finish():
            for copy in copies:
                copy.wait()
            total = acc[:, mine]
            for i in range(3):
                total = total + decoded(part_code[step, i], part_peak[step, i])
            return total

        return finish

    def gather(step, value):
        code, peak = coded(value)
        own_code[step] = code
        own_peak[step] = peak
        copies = []
        for i in range(1, 4):
            _, device = g_peer(i)
            for n, (source, target) in enumerate(((own_code, full_code), (own_peak, full_peak))):
                copies.append(
                    send(
                        source.at[step],
                        target.at[step, g],
                        13 + 2 * i + n,
                        full_sem.at[step, i - 1, n],
                        device,
                    )
                )
        full[:, mine] = value

        def finish():
            for copy in copies:
                copy.wait()
            for i in range(1, 4):
                t, _ = g_peer(i)
                full[:, pl.ds(pl.multiple_of(t * 64, 64), 64)] = decoded(
                    full_code[step, t], full_peak[step, t]
                )

        return finish

    def forward_pair(pair, energy):
        d_real, d_imag = full[0], full[1]
        pieces = []
        for n in range(2):
            real, imag = maps_of(2 * pair + n)
            pieces.append(
                jnp.concatenate(
                    [real * d_real - imag * d_imag, real * d_imag + imag * d_real], axis=1
                )
            )
        sides = split_rows(table_right(jnp.concatenate(pieces, axis=0), fz_ref))
        for p in range(2):
            mask = mask_t[128 * p : 128 * p + 128]
            mask = jnp.concatenate([mask, mask], axis=1)
            mask = jnp.concatenate([mask, mask], axis=0)
            spectrum = table_left(fy_ref[p], sides[p]) * mask
            squares = spectrum * spectrum
            energy = energy + folded(squares[:, :128] + squares[:, 128:])
            high, low = halves(spectrum)
            spectra[pair, p, 0] = high
            spectra[pair, p, 1] = low
        return energy

    def inverse_pair(pair, _):
        sides = []
        for p in range(2):
            high, low = spectra[pair, p, 0], spectra[pair, p, 1]
            sides.append(mm(gy_ref[p, 0], high) + (mm(gy_ref[p, 1], high) + mm(gy_ref[p, 0], low)))
        add_image(table_right(join_rows(*sides), gz_ref), pair)
        return 0

    stages = (
        (8, slab_peer, slab, stat_a, stat_sem_a),
        (4, y_peer, y, stat_b, stat_sem_b),
        (8, line_peer, line, stat_c, stat_sem_c),
    )

    def totals(step, stage, value):
        count, peer, here, slots, sems = stages[stage]
        stat_own[step, stage] = value
        slots[step, pl.ds(here, 1)] = value[None]
        copies = []
        for i in range(1, count):
            copies.append(
                send(
                    stat_own.at[step, stage],
                    slots.at[step, here],
                    7 + i,
                    sems.at[step, i - 1],
                    peer(i)[1],
                )
            )

        def finish():
            for copy in copies:
                copy.wait()
            value = slots[step, 0]
            for i in range(1, count):
                value = value + slots[step, i]
            return value

        return finish

    def norm_of(value):
        return folded((value * value).reshape(128, 128))

    def operator(step, direction):
        finish = gather(step, direction)
        norm = norm_of(direction)
        finish()
        energy = lax.fori_loop(0, 4, forward_pair, jnp.zeros((8, 128), f32))
        acc[...] = jnp.zeros_like(acc)
        finish = totals(step, 0, jnp.stack([norm, energy]))
        lax.fori_loop(0, 2, inverse_pair, 0)
        finish = totals(step, 1, finish())
        lax.fori_loop(2, 4, inverse_pair, 0)
        image = reduce_scatter(step + 1)
        finish = totals(step, 2, finish())
        value = finish()
        norm, energy = jnp.sum(value[0]), jnp.sum(value[1])
        return norm, energy + penalty * norm, image() + penalty * direction

    right = reduce_scatter(0)()
    bulk_wait(2, dsrc, dbuf)
    right = right + penalty * jnp.stack([dbuf[:, 0], dbuf[:, 1]])
    rr, curvature, image = operator(0, right)
    alpha = rr / curvature
    residual = right - alpha * image
    fresh, curvature, second = operator(1, residual)
    growth = fresh / rr
    step_size = fresh / (curvature - growth * fresh / alpha)
    q = second + growth * image
    answer = alpha * right + step_size * (residual + growth * right)
    rest = residual - step_size * q
    for c in range(2):
        osrc[:, c] = answer[c]
        osrc[:, 2 + c] = rest[c]
    bulk((3, osrc, obuf))
    obuf[pl.ds(me, 1)] = osrc[pl.ds(me, 1)]
    bulk_wait(3, osrc, obuf)
    out_ref[0] = jnp.transpose(jnp.concatenate([obuf[:, 0], obuf[:, 1]], axis=0))
    out_ref[1] = jnp.transpose(jnp.concatenate([obuf[:, 2], obuf[:, 3]], axis=0))


def body(
    prior_image,
    coil_maps,
    kspace,
    sampling,
    weight_first,
    bias_first,
    weight_middle,
    bias_middle,
    weight_last,
    bias_last,
):
    mask = sampling.astype(bf16).reshape(16, 128, 2).transpose(0, 2, 1).reshape(16, 256)
    spectrum = kspace[0].reshape(16, 128, 2, 2, 64).transpose(4, 3, 0, 2, 1).reshape(64, 2, 16, 256)
    maps = coil_maps[0].reshape(4, 4, 2, 128, 2, 64).transpose(5, 4, 1, 0, 2, 3)
    maps = maps.reshape(64, 2, 4, 8, 128)
    prior = prior_image.reshape(2, 64, 2, 64).transpose(2, 1, 0, 3).reshape(2, 8192)

    first = weight_first.transpose(1, 2, 0, 4, 3).reshape(9, 6, 32)
    pieces = [jnp.pad(first, ((0, 0), (2 * r, 10 - 2 * r), (0, 0))) for r in (0, 1, 2, 3, 4, 4, 4)]
    w1 = jnp.pad(jnp.concatenate(pieces, axis=2), ((0, 0), (0, 0), (0, 32))).reshape(144, 256)
    middle = weight_middle.transpose(1, 0, 4, 2, 3).reshape(3, 96, 3, 32)
    pieces = [jnp.pad(middle, ((0, 0), (32 * r, 64 - 32 * r), (0, 0), (0, 0))) for r in range(3)]
    middle = jnp.concatenate(pieces + [jnp.zeros_like(pieces[0])], axis=3).reshape(3, 160, 384)
    w2 = jnp.concatenate(
        [
            middle[:, :128].reshape(384, 384),
            middle[:, 128:].reshape(96, 384),
            jnp.zeros((32, 384), bf16),
        ],
        axis=0,
    )
    w3 = weight_last.transpose(1, 2, 3, 0, 4).reshape(9, 2, 96)
    w3 = jnp.pad(w3, ((0, 0), (0, 6), (0, 32))).reshape(72, 128)
    b1 = bias_first[None]
    b2 = bias_middle[None]

    forward, backward, z_forward, z_backward = tables()
    vmem = pl.BlockSpec(memory_space=pltpu.VMEM)
    hbm = pl.BlockSpec(memory_space=pl.ANY)
    out = jax.ShapeDtypeStruct((2, 128, 128), f32)
    smem = pl.BlockSpec(memory_space=pltpu.SMEM)
    dma = pltpu.SemaphoreType.DMA
    out = pl.pallas_call(
        step_kernel,
        out_shape=out,
        in_specs=[vmem] + [hbm] * 2 + [vmem] * 6 + [smem] + [vmem] * 4,
        out_specs=vmem,
        scratch_shapes=[
            pltpu.VMEM((64, 2, 16, 256), bf16),
            pltpu.VMEM((64, 2, 4, 8, 128), bf16),
            pltpu.VMEM((8, 2, 256, 128), f32),
            pltpu.VMEM((2, 8192), bf16),
            pltpu.VMEM((7, 2, 8192), bf16),
            pltpu.VMEM((16, 8192), f32),
            pltpu.VMEM((144, 8192), bf16),
            pltpu.VMEM((8448, 128), bf16),
            pltpu.VMEM((8448, 128), bf16),
            pltpu.VMEM((72, 8192), f32),
            pltpu.VMEM((2, 64, 128), f32),
            pltpu.VMEM((64, 2, 128), f32),
            pltpu.VMEM((64, 2, 128), f32),
            pltpu.VMEM((64, 4, 128), f32),
            pltpu.VMEM((64, 4, 128), f32),
            pltpu.VMEM((2, 256, 128), f32),
            pltpu.VMEM((8, 16, 256), bf16),
            pltpu.VMEM((256, 128), f32),
            pltpu.VMEM((4, 2, 2, 256, 256), bf16),
            pltpu.VMEM((3, 3, 2, 64, 128), jnp.int16),
            pltpu.VMEM((3, 3, 2, 128), f32),
            pltpu.VMEM((3, 3, 2, 64, 128), jnp.int16),
            pltpu.VMEM((3, 3, 2, 128), f32),
            pltpu.VMEM((2, 2, 64, 128), jnp.int16),
            pltpu.VMEM((2, 2, 128), f32),
            pltpu.VMEM((2, 4, 2, 64, 128), jnp.int16),
            pltpu.VMEM((2, 4, 2, 128), f32),
            pltpu.VMEM((2, 256, 128), f32),
            pltpu.VMEM((2, 8, 2, 8, 128), f32),
            pltpu.VMEM((2, 4, 2, 8, 128), f32),
            pltpu.VMEM((2, 8, 2, 8, 128), f32),
            pltpu.VMEM((2, 3, 2, 8, 128), f32),
            dma((22,)),
            dma((3, 3, 2)),
            dma((2, 3, 2)),
            dma((7,)),
            dma((2, 7)),
            dma((2, 3)),
            dma((2, 7)),
            dma((6,)),
            dma((6,)),
            dma((4,)),
            dma((4,)),
            dma((2,)),
        ],
        compiler_params=pltpu.CompilerParams(
            collective_id=0, has_side_effects=True, vmem_limit_bytes=60 * 1024 * 1024
        ),
    )(
        prior,
        spectrum,
        maps,
        mask,
        w1,
        w2,
        w3,
        b1,
        b2,
        bias_last,
        jnp.asarray(forward),
        jnp.asarray(backward),
        jnp.asarray(z_forward),
        jnp.asarray(z_backward),
    )
    return out[0:1], out[1:2]


def solution(mesh):
    torus = Mesh(mesh.devices.reshape(SIZES), AXES)
    coil = ("y", "g", "b")
    slab = ("x", "k")
    in_specs = (
        P(ALL, None, None),
        P(coil, slab, None, None),
        P(coil, slab, None, None),
        P(slab, None),
        P(),
        P(),
        P(),
        P(),
        P(),
        P(),
    )
    out_specs = (P(ALL, None, None), P(ALL, None, None))
    return jax.shard_map(body, mesh=torus, in_specs=in_specs, out_specs=out_specs, check_vma=False)
```

time: 146 us -> 126 us (0.86)
  Pallas kernels: 129 us -> 107 us
  local copies, waits for them, and re-layouts: 12.8 us -> 16.8 us
  other arithmetic: 3.27 us -> 1.08 us
    pallas_call x1, Pallas kernels: 129 us -> 107 us  [body(): pl.pallas_call(step_kernel, out_shape=out, in_specs=[vmem] + [hbm] * 2 +...]
    unnamed x26 -> x14, local copies, waits for them, and re-layouts: 5.53 us -> 1.68 us
    another operation x4 -> x1, local copies, waits for them, and re-layouts: 1.18 us -> 3.87 us  [body(): kspace[0].reshape(16, 128, 2, 2, 64).transpose(4, 3, 0, 2, 1)]
    transpose x0 -> x2, local copies, waits for them, and re-layouts: none -> 1.94 us  [the longest x1 1.87 us: body(): kspace[0].reshape(16, 128, 2, 2, 64).transpose(4, 3, 0, 2, 1)]
    transpose x1 -> x0, other arithmetic: 1.55 us -> none  [body(): spectrum = measured.reshape(16, 256, 2, 64).transpose(3, 2, 0, 1)]
    slice x0 -> x1, local copies, waits for them, and re-layouts: none -> 1.53 us  [body(): return (out[0:1], out[1:2])]
    reshape x0 -> x1, local copies, waits for them, and re-layouts: none -> 1.49 us  [body(): kspace[0].reshape(16, 128, 2, 2, 64).transpose(4, 3, 0, 2, 1)]
where the time goes in v3:
time: 126 us
  Pallas kernels  107 us (85%)
  local copies, waits for them, and re-layouts  16.8 us (13%)
    pallas_call x1, Pallas kernels, body(): pl.pallas_call(step_kernel, out_shape=out, in_specs=[vmem] + [hbm] * 2 +...  107 us
    another operation x1, local copies, waits for them, and re-layouts, body(): kspace[0].reshape(16, 128, 2, 2, 64).transpose(4, 3, 0, 2, 1)  3.87 us

profile of v3, /device:TPU:1, one launch (start us, length us, event | category | flops | bytes accessed | tf_op | source)
XLA Modules:
  0.0 126.0 jit_solution(4501148603844589737)
XLA Ops:
  0.6 1.0 reshape.46
  1.6 0.1 copy.36
  1.7 0.8 reshape.47.prior_ref
  2.5 3.9 %reshape_squeeze.6 = bf16[16,128,2,2,64]{4,3,2,1,0:T(2,128)(2,1)S(1)} reshape(bf16[1,16,256,128]{3,2,1,0:T(8,128)(2,1)} %param.16) | data formatting | bytes 2097152 | tf_op jit(solution)/shard_map/reshape;squeeze | solution.py:641
  6.4 1.9 %copy.21 = bf16[64,2,16,2,128]{4,3,2,1,0:T(2,128)(2,1)S(1)} copy(bf16[64,2,16,2,128]{0,1,3,4,2:T(2,128)(2,1)S(1)} %bitcast.30) | data formatting | bytes 2097152 | tf_op jit(solution)/shard_map/transpose | solution.py:641
  8.3 0.0 copy-start
  8.3 1.5 %reshape.48.k_hbm = bf16[64,2,16,256]{3,2,1,0:T(8,128)(2,1)} reshape(bf16[64,2,16,2,128]{4,3,2,1,0:T(2,128)(2,1)S(1)} %copy.21) | data formatting | bytes 2097152 | tf_op jit(solution)/shard_map/reshape | solution.py:641
  9.8 0.7 copy.22
  10.4 0.0 copy-start.2
  10.4 0.0 copy-start.3
  10.5 0.0 copy-start.1
  10.5 2.1 %copy.23 = bf16[64,2,4,4,2,128]{5,4,3,2,1,0:T(2,128)(2,1)} copy(bf16[64,2,4,4,2,128]{5,0,1,4,2,3:T(8,128)(2,1)S(1)} %bitcast.32) | data formatting | bytes 2097152 | tf_op jit(solution)/shard_map/transpose | solution.py:642
  12.6 0.1 copy.24
  12.7 0.1 copy.25
  12.8 0.6 copy.37
  13.5 0.1 concatenate.9
  13.7 0.6 pad.47
  14.3 0.2 copy.27
  14.5 0.2 reshape.54
  14.6 0.1 pad.58.clone
  14.7 0.2 fusion.6
  14.9 0.1 slice.17
  15.0 0.0 copy-start.4
  15.0 0.2 copy.32
  15.1 0.1 slice.16
  15.2 0.2 copy.31
  15.4 0.1 pad.54.clone
  15.5 0.9 maximum_maximum_fusion.w2_ref
  16.4 0.1 reshape.58
  16.5 0.6 pad_bitcast_fusion.w3_ref
  17.1 107.4 %shard_map.149 = f32[2,128,128]{2,1,0:T(8,128)} custom-call(f32[2,8192]{1,0:T(2,128)} %reshape.47.prior_ref, bf16[64,2,16,256]{3,2,1,0:T(8,128)(2,1)} %reshape.48.k_hbm, bf16[64,2,4,8,128]{4,3,2,1,0:T(8,128)(2,1)} %bitcast.31, bf16[16,256]{1,0:T(8,128)(2,1)} %bitcast.41, bf16[144,256]{1,0:T(8,128)(2,1)} %bitcast.38, ...), custom_call_target="tpu_custom_call" | custom-call | tf_op jit(solution)/shard_map/pallas_call | solution.py:671
  124.5 1.5 %fusion.8 = (f32[1,128,128]{2,1,0:T(8,128)}, f32[1,128,128]{2,1,0:T(8,128)}) fusion(f32[2,128,128]{2,1,0:T(8,128)} %shard_map.149), kind=kLoop, calls=%fused_computation.17 | loop fusion | bytes 262144 | tf_op jit(solution)/shard_map/slice | solution.py:741
  (11 shorter events, 0.1 us)
Async XLA Ops:
  8.3 1.5 %copy-start = (bf16[1,32,128,128]{3,2,1,0:T(8,128)(2,1)S(1)}, bf16[1,32,128,128]{3,2,1,0:T(8,128)(2,1)}, u32[]{:S(2)}) copy-start(bf16[1,32,128,128]{3,2,1,0:T(8,128)(2,1)} %param.15) | copy-start | bytes 3145732
  10.4 2.2 %copy-start.2 = (s32[16,256]{1,0:T(8,128)S(1)}, s32[16,256]{1,0:T(8,128)}, u32[]{:S(2)}) copy-start(s32[16,256]{1,0:T(8,128)} %param.17) | copy-start | bytes 49156
  10.4 3.0 %copy-start.3 = (bf16[3,3,3,32,2]{3,4,2,1,0:T(2,128)(2,1)S(1)}, bf16[3,3,3,32,2]{3,4,2,1,0:T(2,128)(2,1)}, u32[]{:S(2)}) copy-start(bf16[3,3,3,32,2]{3,4,2,1,0:T(2,128)(2,1)} %param.18) | copy-start | bytes 10372
  10.5 3.8 %copy-start.1 = (bf16[3,3,3,32,32]{4,3,2,1,0:T(8,128)(2,1)S(1)}, bf16[3,3,3,32,32]{4,3,2,1,0:T(8,128)(2,1)}, u32[]{:S(2)}) copy-start(bf16[3,3,3,32,32]{4,3,2,1,0:T(8,128)(2,1)} %param.20) | copy-start | bytes 165892
  15.0 1.4 %copy-start.4 = (bf16[3,3,3,2,32]{4,3,2,1,0:T(2,128)(2,1)S(1)}, bf16[3,3,3,2,32]{4,3,2,1,0:T(2,128)(2,1)}, u32[]{:S(2)}) copy-start(bf16[3,3,3,2,32]{4,3,2,1,0:T(2,128)(2,1)} %param.22) | copy-start | bytes 10372

commit v4 on v3

--- a/solution.py
+++ b/solution.py
@@ -61,36 +61,8 @@
     return jnp.dot(a, b, preferred_element_type=f32)
 
 
-def table_right(value, table):
-    high, low = halves(value)
-    return mm(high, table[0]) + (mm(high, table[1]) + mm(low, table[0]))
-
-
-def table_left(table, value):
-    high, low = halves(value)
-    return mm(table[0], high) + (mm(table[1], high) + mm(table[0], low))
-
-
-def split_rows(value):
-    sums, differences = [], []
-    for n in range(2):
-        low = jnp.concatenate([value[256 * n + 64 * h :][:32] for h in range(4)], axis=0)
-        high = jnp.concatenate([value[256 * n + 64 * h + 32 :][:32] for h in range(4)], axis=0)
-        for out, part in ((sums, low + high), (differences, low - high)):
-            out.append(jnp.concatenate([part[:, :128], part[:, 128:]], axis=0))
-    return jnp.concatenate(sums, axis=1), jnp.concatenate(differences, axis=1)
-
-
-def join_rows(even, odd):
-    low, high = even + odd, even - odd
-    pieces = []
-    for n in range(2):
-        first = slice(128 * n, 128 * n + 128)
-        parts = [jnp.concatenate([p[:128, first], p[128:, first]], axis=1) for p in (low, high)]
-        for h in range(4):
-            for part in parts:
-                pieces.append(part[32 * h : 32 * h + 32])
-    return jnp.concatenate(pieces, axis=0)
+def three(left, right):
+    return mm(left[0], right[0]) + (mm(left[0], right[1]) + mm(left[1], right[0]))
 
 
 def coded(value):
@@ -147,7 +119,7 @@
     prior_ref,
     k_hbm,
     m_hbm,
-    mask_ref,
+    sampling_ref,
     w1_ref,
     w2_ref,
     w3_ref,
@@ -162,6 +134,8 @@
     k_ref,
     m_ref,
     s_ref,
+    cells,
+    flat,
     feat,
     fbuf,
     f_rows,
@@ -174,10 +148,12 @@
     dbuf,
     osrc,
     obuf,
-    acc,
+    mask_own,
     mask_all,
     mask_t,
+    rows_in,
     spectra,
+    rows_out,
     out_code,
     out_peak,
     part_code,
@@ -186,7 +162,6 @@
     own_peak,
     full_code,
     full_peak,
-    full,
     stat_a,
     stat_b,
     stat_c,
@@ -257,7 +232,15 @@
                 device_id={"g": lax.rem(g + i, 4), "b": lax.rem(b + c, 2)},
                 device_id_type=mesh_id,
             )
-    feat[...] = prior_ref[...].astype(bf16)
+    mask_own[...] = sampling_ref[...].astype(f32).astype(bf16)
+    left = lanes((64, 128)) < 64
+    top, bottom = prior_ref[0:64], prior_ref[64:128]
+    cells[0] = jnp.where(left, top, pltpu.roll(bottom, 64, 1))
+    cells[1] = jnp.where(left, pltpu.roll(top, 64, 1), bottom)
+    for i in range(64):
+        for c in range(2):
+            flat[c : c + 1, 128 * i : 128 * i + 128] = cells[c, i : i + 1]
+    feat[...] = flat[...].astype(bf16)
     k_local = pltpu.make_async_copy(k_hbm.at[me], k_ref.at[me], local_sem.at[0])
     m_local = pltpu.make_async_copy(m_hbm.at[me], m_ref.at[me], local_sem.at[1])
     k_local.start()
@@ -302,9 +285,9 @@
     mask_copies = []
     for i in range(1, 8):
         mask_copies.append(
-            send(mask_ref, mask_all.at[slab], i - 1, mask_sem.at[i - 1], slab_peer(i)[1])
+            send(mask_own, mask_all.at[slab], i - 1, mask_sem.at[i - 1], slab_peer(i)[1])
         )
-    mask_all[pl.ds(slab, 1)] = mask_ref[...][None]
+    mask_all[pl.ds(slab, 1)] = mask_own[...][None]
     bulk((0, k_hbm, k_ref), (1, m_hbm, m_ref))
 
     fbuf[3] = feat[...]
@@ -390,58 +373,57 @@
             tap = dz * 3 + dx
             side = side + plane_shift(p3[8 * tap : 8 * tap + 8], dz - 1)
         total = total + column_shift(side, dx - 1)
-    channel = lax.broadcasted_iota(jnp.int32, (2, 1), 0)
-    total = total[0:2] + (prior_ref[...] + jnp.where(channel == 0, b3_ref[0], b3_ref[1]))
     for i in range(64):
         for c in range(2):
             dplanes[c, i : i + 1] = total[c : c + 1, 128 * i : 128 * i + 128]
     for c in range(2):
-        turned = jnp.transpose(dplanes[c])
+        turned = jnp.transpose(dplanes[c] + (cells[c] + b3_ref[c]))
         dsrc[:, c] = jnp.concatenate([turned[:64], turned[64:]], axis=1)
     bulk((2, dsrc, dbuf))
     dbuf[pl.ds(me, 1)] = dsrc[pl.ds(me, 1)]
 
-    acc[...] = jnp.zeros_like(acc)
-
-    def maps_of(j):
-        return s_ref[j, 0], s_ref[j, 1]
-
-    def add_image(image, pair):
-        for n in range(2):
-            real, imag = maps_of(2 * pair + n)
-            a_real = image[256 * n : 256 * n + 256, :128]
-            a_imag = image[256 * n : 256 * n + 256, 128:]
-            acc[0] += real * a_real + imag * a_imag
-            acc[1] += real * a_imag - imag * a_real
-
     k_local.wait()
     m_local.wait()
+    for copy in mask_copies:
+        copy.wait()
+    order = lax.broadcasted_iota(jnp.int32, (256, 256), 0)
+    order = 2 * lax.rem(order, 128) + order // 128
+    order = (order == lax.broadcasted_iota(jnp.int32, (256, 256), 1)).astype(bf16)
+    mask_rows = mask_all[...].reshape(128, 256)
+    by_line = (((1,), (1,)), ((), ()))
+    mask_t[...] = lax.dot_general(order, mask_rows, by_line, preferred_element_type=f32)
     bulk_wait(0, k_hbm, k_ref)
     bulk_wait(1, m_hbm, m_ref)
 
-    for copy in mask_copies:
-        copy.wait()
-    half = lax.broadcasted_iota(jnp.int32, (256, 256), 0)
-    eye = (half == lax.broadcasted_iota(jnp.int32, (256, 256), 1)).astype(bf16)
-    mask_rows = mask_all[...].reshape(128, 256)
-    by_line = (((1,), (1,)), ((), ()))
-    mask_t[...] = lax.dot_general(eye, mask_rows, by_line, preferred_element_type=f32)
+    def put_rows(pair, even, odd):
+        for h, part in ((0, even + odd), (1, even - odd)):
+            for q, value in enumerate(halves(part)):
+                for n in range(2):
+                    first = slice(128 * n, 128 * n + 128)
+                    piece = jnp.concatenate([value[:128, first], value[128:, first]], axis=1)
+                    for i in range(4):
+                        rows_out[q, i, 2 * pair + n, 32 * h : 32 * h + 32] = piece[
+                            32 * i : 32 * i + 32
+                        ]
 
     def adjoint_pair(pair, _):
+        planes = []
+        for n in range(2):
+            for c in range(2):
+                plane = jnp.concatenate(
+                    [k_ref[8 * s + 2 * pair + n, c] for s in range(8)], axis=0
+                )
+                planes.append(plane * mask_rows)
+        planes = lax.dot_general(
+            jnp.concatenate(planes, axis=0), order, by_line, preferred_element_type=f32
+        ).astype(bf16)
         sides = []
         for p in range(2):
-            cells = slice(128 * p, 128 * p + 128)
-            planes = []
-            for n in range(2):
-                for c in range(2):
-                    plane = jnp.concatenate(
-                        [k_ref[8 * s + 2 * pair + n, c][:, cells] for s in range(8)], axis=0
-                    )
-                    planes.append(plane * mask_rows[:, cells])
+            cell = slice(128 * p, 128 * p + 128)
             spectrum = jnp.concatenate(
                 [
-                    jnp.concatenate(planes[0:2], axis=1),
-                    jnp.concatenate(planes[2:4], axis=1),
+                    jnp.concatenate([planes[0:128, cell], planes[128:256, cell]], axis=1),
+                    jnp.concatenate([planes[256:384, cell], planes[384:512, cell]], axis=1),
                 ],
                 axis=0,
             )
@@ -449,6 +431,7 @@
                 lax.dot_general(gy_ref[p, 0], spectrum, by_line, preferred_element_type=f32)
                 + lax.dot_general(gy_ref[p, 1], spectrum, by_line, preferred_element_type=f32)
             )
+        put_rows(pair, *sides)
         for n in range(2):
             j = 2 * pair + n
             for c in range(2):
@@ -456,18 +439,31 @@
                     for s in range(8):
                         first = h * 64 + s * 8
                         s_ref[j, c, first : first + 8] = m_ref[8 * s + j, c, h].astype(f32)
-        add_image(table_right(join_rows(*sides), gz_ref), pair)
         return 0
 
-    lax.fori_loop(0, 4, adjoint_pair, 0)
-
-    mine = pl.ds(pl.multiple_of(g * 64, 64), 64)
-
-    def reduce_scatter(step):
+    lax.fori_loop(0, 4, adjoint_pair, 0, unroll=2)
+
+    def maps_of(j, h):
+        rows = pl.ds(pl.multiple_of(h * 64, 64), 64)
+        return s_ref[j, 0, rows], s_ref[j, 1, rows]
+
+    def image_rows(h):
+        left = rows_out[0, h].reshape(512, 256), rows_out[1, h].reshape(512, 256)
+        image = three(left, (gz_ref[0], gz_ref[1]))
+        real_total, imag_total = 0.0, 0.0
+        for j in range(8):
+            real, imag = maps_of(j, h)
+            a_real = image[64 * j : 64 * j + 64, :128]
+            a_imag = image[64 * j : 64 * j + 64, 128:]
+            real_total = real_total + (real * a_real + imag * a_imag)
+            imag_total = imag_total + (real * a_imag - imag * a_real)
+        return jnp.stack([real_total, imag_total])
+
+    def reduce_scatter(step, between=lambda: None):
         copies = []
-        for i in range(1, 4):
+        for i in (2, 1, 3):
             t, device = g_peer(i)
-            code, peak = coded(acc[:, pl.ds(pl.multiple_of(t * 64, 64), 64)])
+            code, peak = coded(image_rows(t))
             out_code[step, i - 1] = code
             out_peak[step, i - 1] = peak
             for n, (source, target) in enumerate(((out_code, part_code), (out_peak, part_peak))):
@@ -480,14 +476,16 @@
                         device,
                     )
                 )
+        between()
+        total = image_rows(g)
 
         def finish():
             for copy in copies:
                 copy.wait()
-            total = acc[:, mine]
+            value = total
             for i in range(3):
-                total = total + decoded(part_code[step, i], part_peak[step, i])
-            return total
+                value = value + decoded(part_code[step, i], part_peak[step, i])
+            return value
 
         return finish
 
@@ -495,48 +493,57 @@
         code, peak = coded(value)
         own_code[step] = code
         own_peak[step] = peak
-        copies = []
-        for i in range(1, 4):
+        copies = {}
+        for i in (2, 1, 3):
             _, device = g_peer(i)
-            for n, (source, target) in enumerate(((own_code, full_code), (own_peak, full_peak))):
-                copies.append(
-                    send(
-                        source.at[step],
-                        target.at[step, g],
-                        13 + 2 * i + n,
-                        full_sem.at[step, i - 1, n],
-                        device,
-                    )
+            copies[i] = [
+                send(
+                    source.at[step],
+                    target.at[step, g],
+                    13 + 2 * i + n,
+                    full_sem.at[step, i - 1, n],
+                    device,
                 )
-        full[:, mine] = value
-
-        def finish():
-            for copy in copies:
+                for n, (source, target) in enumerate(((own_code, full_code), (own_peak, full_peak)))
+            ]
+
+        def finish(i):
+            for copy in copies[i]:
                 copy.wait()
-            for i in range(1, 4):
-                t, _ = g_peer(i)
-                full[:, pl.ds(pl.multiple_of(t * 64, 64), 64)] = decoded(
-                    full_code[step, t], full_peak[step, t]
-                )
+            t = lax.rem(g + 4 - i, 4)
+            return t, decoded(full_code[step, t], full_peak[step, t])
 
         return finish
 
-    def forward_pair(pair, energy):
-        d_real, d_imag = full[0], full[1]
+    def forward_rows(h, value):
         pieces = []
-        for n in range(2):
-            real, imag = maps_of(2 * pair + n)
+        for j in range(8):
+            real, imag = maps_of(j, h)
             pieces.append(
                 jnp.concatenate(
-                    [real * d_real - imag * d_imag, real * d_imag + imag * d_real], axis=1
+                    [
+                        real * value[0] - imag * value[1],
+                        real * value[1] + imag * value[0],
+                    ],
+                    axis=1,
                 )
             )
-        sides = split_rows(table_right(jnp.concatenate(pieces, axis=0), fz_ref))
+        lines = three(halves(jnp.concatenate(pieces, axis=0)), (fz_ref[0], fz_ref[1]))
+        for j in range(8):
+            low, high = lines[64 * j : 64 * j + 32], lines[64 * j + 32 : 64 * j + 64]
+            place = slice(128 * (j % 2), 128 * (j % 2) + 128)
+            for p, part in enumerate((low + high, low - high)):
+                for q, piece in enumerate(halves(part)):
+                    for c in range(2):
+                        rows_in[q, j // 2, p, c, h, :, place] = piece[:, 128 * c : 128 * c + 128]
+
+    def forward_pair(pair, energy):
         for p in range(2):
             mask = mask_t[128 * p : 128 * p + 128]
             mask = jnp.concatenate([mask, mask], axis=1)
             mask = jnp.concatenate([mask, mask], axis=0)
-            spectrum = table_left(fy_ref[p], sides[p]) * mask
+            sides = [rows_in[q, pair, p].reshape(256, 256) for q in range(2)]
+            spectrum = three((fy_ref[p, 0], fy_ref[p, 1]), sides) * mask
             squares = spectrum * spectrum
             energy = energy + folded(squares[:, :128] + squares[:, 128:])
             high, low = halves(spectrum)
@@ -547,9 +554,9 @@
     def inverse_pair(pair, _):
         sides = []
         for p in range(2):
-            high, low = spectra[pair, p, 0], spectra[pair, p, 1]
-            sides.append(mm(gy_ref[p, 0], high) + (mm(gy_ref[p, 1], high) + mm(gy_ref[p, 0], low)))
-        add_image(table_right(join_rows(*sides), gz_ref), pair)
+            right = spectra[pair, p, 0], spectra[pair, p, 1]
+            sides.append(three((gy_ref[p, 0], gy_ref[p, 1]), right))
+        put_rows(pair, *sides)
         return 0
 
     stages = (
@@ -590,16 +597,18 @@
     def operator(step, direction):
         finish = gather(step, direction)
         norm = norm_of(direction)
-        finish()
-        energy = lax.fori_loop(0, 4, forward_pair, jnp.zeros((8, 128), f32))
-        acc[...] = jnp.zeros_like(acc)
-        finish = totals(step, 0, jnp.stack([norm, energy]))
-        lax.fori_loop(0, 2, inverse_pair, 0)
-        finish = totals(step, 1, finish())
-        lax.fori_loop(2, 4, inverse_pair, 0)
-        image = reduce_scatter(step + 1)
-        finish = totals(step, 2, finish())
-        value = finish()
+        forward_rows(g, direction)
+        for i in (1, 3, 2):
+            forward_rows(*finish(i))
+        energy = lax.fori_loop(0, 4, forward_pair, jnp.zeros((8, 128), f32), unroll=2)
+        finish_a = totals(step, 0, jnp.stack([norm, energy]))
+        lax.fori_loop(0, 4, inverse_pair, 0, unroll=2)
+        finish_b = totals(step, 1, finish_a())
+        last = []
+        image = reduce_scatter(
+            step + 1, lambda: last.append(totals(step, 2, finish_b()))
+        )
+        value = last[0]()
         norm, energy = jnp.sum(value[0]), jnp.sum(value[1])
         return norm, energy + penalty * norm, image() + penalty * direction
 
@@ -637,11 +646,9 @@
     weight_last,
     bias_last,
 ):
-    mask = sampling.astype(bf16).reshape(16, 128, 2).transpose(0, 2, 1).reshape(16, 256)
-    spectrum = kspace[0].reshape(16, 128, 2, 2, 64).transpose(4, 3, 0, 2, 1).reshape(64, 2, 16, 256)
+    spectrum = kspace[0].reshape(16, 256, 2, 64).transpose(3, 2, 0, 1)
     maps = coil_maps[0].reshape(4, 4, 2, 128, 2, 64).transpose(5, 4, 1, 0, 2, 3)
     maps = maps.reshape(64, 2, 4, 8, 128)
-    prior = prior_image.reshape(2, 64, 2, 64).transpose(2, 1, 0, 3).reshape(2, 8192)
 
     first = weight_first.transpose(1, 2, 0, 4, 3).reshape(9, 6, 32)
     pieces = [jnp.pad(first, ((0, 0), (2 * r, 10 - 2 * r), (0, 0))) for r in (0, 1, 2, 3, 4, 4, 4)]
@@ -677,6 +684,8 @@
             pltpu.VMEM((64, 2, 16, 256), bf16),
             pltpu.VMEM((64, 2, 4, 8, 128), bf16),
             pltpu.VMEM((8, 2, 256, 128), f32),
+            pltpu.VMEM((2, 64, 128), f32),
+            pltpu.VMEM((2, 8192), f32),
             pltpu.VMEM((2, 8192), bf16),
             pltpu.VMEM((7, 2, 8192), bf16),
             pltpu.VMEM((16, 8192), f32),
@@ -689,10 +698,12 @@
             pltpu.VMEM((64, 2, 128), f32),
             pltpu.VMEM((64, 4, 128), f32),
             pltpu.VMEM((64, 4, 128), f32),
-            pltpu.VMEM((2, 256, 128), f32),
+            pltpu.VMEM((16, 256), bf16),
             pltpu.VMEM((8, 16, 256), bf16),
             pltpu.VMEM((256, 128), f32),
+            pltpu.VMEM((2, 4, 2, 2, 4, 32, 256), bf16),
             pltpu.VMEM((4, 2, 2, 256, 256), bf16),
+            pltpu.VMEM((2, 4, 8, 64, 256), bf16),
             pltpu.VMEM((3, 3, 2, 64, 128), jnp.int16),
             pltpu.VMEM((3, 3, 2, 128), f32),
             pltpu.VMEM((3, 3, 2, 64, 128), jnp.int16),
@@ -701,7 +712,6 @@
             pltpu.VMEM((2, 2, 128), f32),
             pltpu.VMEM((2, 4, 2, 64, 128), jnp.int16),
             pltpu.VMEM((2, 4, 2, 128), f32),
-            pltpu.VMEM((2, 256, 128), f32),
             pltpu.VMEM((2, 8, 2, 8, 128), f32),
             pltpu.VMEM((2, 4, 2, 8, 128), f32),
             pltpu.VMEM((2, 8, 2, 8, 128), f32),
@@ -723,10 +733,10 @@
             collective_id=0, has_side_effects=True, vmem_limit_bytes=60 * 1024 * 1024
         ),
     )(
-        prior,
+        prior_image[0],
         spectrum,
         maps,
-        mask,
+        sampling,
         w1,
         w2,
         w3,

time: 126 us -> 113 us (0.90)
  local copies, waits for them, and re-layouts: 16.8 us -> 9.89 us
  Pallas kernels: 107 us -> 101 us
    pallas_call x1, Pallas kernels: 107 us -> 101 us  [body(): pl.pallas_call(step_kernel, out_shape=out, in_specs=[vmem] + [hbm] * 2 +...]
    reshape x4 -> x0, local copies, waits for them, and re-layouts: 3.36 us -> none  [the longest x3 1.87 us: body(): prior_image.reshape(2, 64, 2, 64).transpose(2, 1, 0, 3).reshape(2, 8192)]
    another operation x1, local copies, waits for them, and re-layouts: 3.87 us -> 1.56 us  [body(): spectrum = kspace[0].reshape(16, 256, 2, 64).transpose(3, 2, 0, 1)]
    transpose x2 -> x0, local copies, waits for them, and re-layouts: 1.94 us -> none  [the longest x1 1.87 us: body(): kspace[0].reshape(16, 128, 2, 2, 64).transpose(4, 3, 0, 2, 1)]
    unnamed x14 -> x12, local copies, waits for them, and re-layouts: 1.68 us -> 2.54 us
where the time goes in v4:
time: 113 us; the launch traced here: 112 us
  Pallas kernels  101 us (89%)
  local copies, waits for them, and re-layouts  9.89 us (9%)
    pallas_call x1, Pallas kernels, body(): pl.pallas_call(step_kernel, out_shape=out, in_specs=[vmem] + [hbm] * 2 +...  101 us
    unnamed x12, local copies, waits for them, and re-layouts  2.54 us

profile of v4, /device:TPU:1, one launch (start us, length us, event | category | flops | bytes accessed | tf_op | source)
XLA Modules:
  0.0 112.4 jit_solution(905721815890029319)
XLA Ops:
  0.6 1.5 %copy.17 = bf16[1,16,256,128]{2,3,1,0:T(8,128)(2,1)S(1)} copy(bf16[1,16,256,128]{3,2,1,0:T(8,128)(2,1)} %param.16) | data formatting | bytes 2097152 | tf_op args[2]
  2.1 0.0 copy-start
  2.1 1.6 %copy.29 = bf16[16,256,2,64]{1,0,2,3:T(8,128)(2,1)} copy(bf16[16,256,2,64]{1,3,2,0:T(8,128)(2,1)S(1)} %bitcast.24) | data formatting | bytes 2097152 | tf_op jit(solution)/shard_map/reshape;squeeze | solution.py:649
  3.7 0.0 copy-done
  3.7 0.7 copy.19
  4.4 0.0 copy-start.2
  4.4 0.0 copy-start.1
  4.4 2.1 %copy.20 = bf16[64,2,4,4,2,128]{5,4,3,2,1,0:T(2,128)(2,1)} copy(bf16[64,2,4,4,2,128]{5,0,1,4,2,3:T(8,128)(2,1)S(1)} %bitcast.25) | data formatting | bytes 2097152 | tf_op jit(solution)/shard_map/transpose | solution.py:650
  6.5 0.0 copy-done.2
  6.6 0.1 concatenate.9
  6.7 0.6 pad.47
  7.4 0.0 copy-done.1
  7.4 0.2 copy.22
  7.5 0.2 reshape.34
  7.7 0.1 pad.58.clone
  7.8 0.2 fusion.6
  8.0 0.1 slice.17
  8.0 0.2 copy.27
  8.2 0.0 copy-start.3
  8.2 0.1 slice.16
  8.3 0.2 copy.26
  8.5 0.1 pad.54.clone
  8.6 0.9 maximum_maximum_fusion.w2_ref
  9.5 0.0 copy-done.3
  9.5 0.1 reshape.38
  9.6 0.6 pad_bitcast_fusion.w3_ref
  10.2 100.7 %shard_map.149 = f32[2,128,128]{2,1,0:T(8,128)} custom-call(f32[128,128]{1,0:T(8,128)} %bitcast.32, bf16[64,2,16,256]{3,2,1,0:T(8,128)(2,1)} %bitcast.22, bf16[64,2,4,8,128]{4,3,2,1,0:T(8,128)(2,1)} %bitcast.23, s32[16,256]{1,0:T(8,128)} %sampling_ref.1, bf16[144,256]{1,0:T(8,128)(2,1)} %bitcast.30, bf16[512,384]{1,0:T(8,128)(2,1)} %maximum_maximum_fusion.w2_ref, ...), custom_call_target="tpu_custom_call" | custom-call | tf_op jit(solution)/shard_map/pallas_call | solution.py:678
  110.8 1.5 %fusion.8 = (f32[1,128,128]{2,1,0:T(8,128)}, f32[1,128,128]{2,1,0:T(8,128)}) fusion(f32[2,128,128]{2,1,0:T(8,128)} %shard_map.149), kind=kLoop, calls=%fused_computation.16 | loop fusion | bytes 262144 | tf_op jit(solution)/shard_map/slice | solution.py:751
  (5 shorter events, 0.1 us)
Async XLA Ops:
  2.1 1.6 %copy-start = (bf16[1,32,128,128]{3,2,1,0:T(8,128)(2,1)S(1)}, bf16[1,32,128,128]{3,2,1,0:T(8,128)(2,1)}, u32[]{:S(2)}) copy-start(bf16[1,32,128,128]{3,2,1,0:T(8,128)(2,1)} %param.15) | copy-start | bytes 3145732
  4.4 2.1 %copy-start.2 = (bf16[3,3,3,32,2]{3,4,2,1,0:T(2,128)(2,1)S(1)}, bf16[3,3,3,32,2]{3,4,2,1,0:T(2,128)(2,1)}, u32[]{:S(2)}) copy-start(bf16[3,3,3,32,2]{3,4,2,1,0:T(2,128)(2,1)} %param.18) | copy-start | bytes 10372
  4.4 3.0 %copy-start.1 = (bf16[3,3,3,32,32]{4,3,2,1,0:T(8,128)(2,1)S(1)}, bf16[3,3,3,32,32]{4,3,2,1,0:T(8,128)(2,1)}, u32[]{:S(2)}) copy-start(bf16[3,3,3,32,32]{4,3,2,1,0:T(8,128)(2,1)} %param.20) | copy-start | bytes 165892
  8.2 1.2 %copy-start.3 = (bf16[3,3,3,2,32]{4,3,2,1,0:T(2,128)(2,1)S(1)}, bf16[3,3,3,2,32]{4,3,2,1,0:T(2,128)(2,1)}, u32[]{:S(2)}) copy-start(bf16[3,3,3,2,32]{4,3,2,1,0:T(2,128)(2,1)} %param.22) | copy-start | bytes 10372

commit v5 on v4

--- a/solution.py
+++ b/solution.py
@@ -163,15 +163,14 @@
     full_code,
     full_peak,
     stat_a,
-    stat_b,
     stat_c,
     stat_own,
     send_sem,
     part_sem,
     full_sem,
     mask_sem,
+    stat_send,
     stat_sem_a,
-    stat_sem_b,
     stat_sem_c,
     feat_send,
     feat_sem,
@@ -204,10 +203,6 @@
     def slab_peer(i):
         t = lax.rem(slab + i, 8)
         return t, {"x": t // 2, "k": lax.rem(t, 2)}
-
-    def y_peer(i):
-        t = lax.rem(y + i, 4)
-        return t, {"y": t}
 
     def line_peer(i):
         t = lax.rem(line + i, 8)
@@ -288,7 +283,8 @@
             send(mask_own, mask_all.at[slab], i - 1, mask_sem.at[i - 1], slab_peer(i)[1])
         )
     mask_all[pl.ds(slab, 1)] = mask_own[...][None]
-    bulk((0, k_hbm, k_ref), (1, m_hbm, m_ref))
+    bulk((0, k_hbm, k_ref))
+    bulk((1, m_hbm, m_ref))
 
     fbuf[3] = feat[...]
     for copy in feat_copies:
@@ -383,7 +379,6 @@
     dbuf[pl.ds(me, 1)] = dsrc[pl.ds(me, 1)]
 
     k_local.wait()
-    m_local.wait()
     for copy in mask_copies:
         copy.wait()
     order = lax.broadcasted_iota(jnp.int32, (256, 256), 0)
@@ -393,7 +388,6 @@
     by_line = (((1,), (1,)), ((), ()))
     mask_t[...] = lax.dot_general(order, mask_rows, by_line, preferred_element_type=f32)
     bulk_wait(0, k_hbm, k_ref)
-    bulk_wait(1, m_hbm, m_ref)
 
     def put_rows(pair, even, odd):
         for h, part in ((0, even + odd), (1, even - odd)):
@@ -432,16 +426,21 @@
                 + lax.dot_general(gy_ref[p, 1], spectrum, by_line, preferred_element_type=f32)
             )
         put_rows(pair, *sides)
-        for n in range(2):
-            j = 2 * pair + n
-            for c in range(2):
-                for h in range(4):
-                    for s in range(8):
-                        first = h * 64 + s * 8
-                        s_ref[j, c, first : first + 8] = m_ref[8 * s + j, c, h].astype(f32)
         return 0
 
     lax.fori_loop(0, 4, adjoint_pair, 0, unroll=2)
+    m_local.wait()
+    bulk_wait(1, m_hbm, m_ref)
+
+    def widen_maps(j, _):
+        for c in range(2):
+            for h in range(4):
+                for s in range(8):
+                    first = h * 64 + s * 8
+                    s_ref[j, c, first : first + 8] = m_ref[8 * s + j, c, h].astype(f32)
+        return 0
+
+    lax.fori_loop(0, 8, widen_maps, 0, unroll=2)
 
     def maps_of(j, h):
         rows = pl.ds(pl.multiple_of(h * 64, 64), 64)
@@ -559,34 +558,59 @@
         put_rows(pair, *sides)
         return 0
 
-    stages = (
-        (8, slab_peer, slab, stat_a, stat_sem_a),
-        (4, y_peer, y, stat_b, stat_sem_b),
-        (8, line_peer, line, stat_c, stat_sem_c),
-    )
-
-    def totals(step, stage, value):
-        count, peer, here, slots, sems = stages[stage]
-        stat_own[step, stage] = value
-        slots[step, pl.ds(here, 1)] = value[None]
+    here = x * 8 + k * 4 + y
+    plane = [
+        {"x": xs[i], "k": ks[j], "y": ys[n]}
+        for n in range(4)
+        for j in range(2)
+        for i in range(4)
+        if i or j or n
+    ]
+
+    def plane_total(step, value):
+        stat_own[step, 0] = value
+        stat_a[step, pl.ds(here, 1)] = value[None]
+        for device in plane:
+            copy_to(
+                stat_own.at[step, 0],
+                stat_a.at[step, here],
+                stat_send.at[step],
+                stat_sem_a.at[step],
+                device,
+            )
+
+        def finish():
+            block = stat_a.at[step, pl.ds(0, 31)]
+            pltpu.make_async_copy(block, block, stat_sem_a.at[step]).wait()
+            pltpu.make_async_copy(block, block, stat_send.at[step]).wait()
+            value = stat_a[step, 0]
+            for i in range(1, 32):
+                value = value + stat_a[step, i]
+            return value
+
+        return finish
+
+    def line_total(step, value):
+        stat_own[step, 1] = value
+        stat_c[step, pl.ds(line, 1)] = value[None]
         copies = []
-        for i in range(1, count):
+        for i in range(1, 8):
             copies.append(
                 send(
-                    stat_own.at[step, stage],
-                    slots.at[step, here],
+                    stat_own.at[step, 1],
+                    stat_c.at[step, line],
                     7 + i,
-                    sems.at[step, i - 1],
-                    peer(i)[1],
+                    stat_sem_c.at[step, i - 1],
+                    line_peer(i)[1],
                 )
             )
 
         def finish():
             for copy in copies:
                 copy.wait()
-            value = slots[step, 0]
-            for i in range(1, count):
-                value = value + slots[step, i]
+            value = stat_c[step, 0]
+            for i in range(1, 8):
+                value = value + stat_c[step, i]
             return value
 
         return finish
@@ -601,15 +625,15 @@
         for i in (1, 3, 2):
             forward_rows(*finish(i))
         energy = lax.fori_loop(0, 4, forward_pair, jnp.zeros((8, 128), f32), unroll=2)
-        finish_a = totals(step, 0, jnp.stack([norm, energy]))
+        stats = [jnp.sum(value, axis=0, keepdims=True) for value in (norm, energy)]
+        finish_plane = plane_total(step, jnp.concatenate(stats, axis=0))
         lax.fori_loop(0, 4, inverse_pair, 0, unroll=2)
-        finish_b = totals(step, 1, finish_a())
         last = []
         image = reduce_scatter(
-            step + 1, lambda: last.append(totals(step, 2, finish_b()))
+            step + 1, lambda: last.append(line_total(step, finish_plane()))
         )
         value = last[0]()
-        norm, energy = jnp.sum(value[0]), jnp.sum(value[1])
+        norm, energy = jnp.sum(value[0:1]), jnp.sum(value[1:2])
         return norm, energy + penalty * norm, image() + penalty * direction
 
     right = reduce_scatter(0)()
@@ -712,16 +736,15 @@
             pltpu.VMEM((2, 2, 128), f32),
             pltpu.VMEM((2, 4, 2, 64, 128), jnp.int16),
             pltpu.VMEM((2, 4, 2, 128), f32),
-            pltpu.VMEM((2, 8, 2, 8, 128), f32),
-            pltpu.VMEM((2, 4, 2, 8, 128), f32),
-            pltpu.VMEM((2, 8, 2, 8, 128), f32),
-            pltpu.VMEM((2, 3, 2, 8, 128), f32),
+            pltpu.VMEM((2, 32, 2, 128), f32),
+            pltpu.VMEM((2, 8, 2, 128), f32),
+            pltpu.VMEM((2, 2, 2, 128), f32),
             dma((22,)),
             dma((3, 3, 2)),
             dma((2, 3, 2)),
             dma((7,)),
-            dma((2, 7)),
-            dma((2, 3)),
+            dma((2,)),
+            dma((2,)),
             dma((2, 7)),
             dma((6,)),
             dma((6,)),

time: 113 us -> 105 us (0.929)
  Pallas kernels: 101 us -> 92.6 us
    pallas_call x1, Pallas kernels: 101 us -> 92.6 us  [body(): pl.pallas_call(step_kernel, out_shape=out, in_specs=[vmem] + [hbm] * 2 +...]
where the time goes in v5:
time: 105 us; the launch traced here: 104 us
  Pallas kernels  92.6 us (88%)
  local copies, waits for them, and re-layouts  9.89 us (9%)
  other arithmetic  1.06 us (1%)
    pallas_call x1, Pallas kernels, body(): pl.pallas_call(step_kernel, out_shape=out, in_specs=[vmem] + [hbm] * 2 +...  92.6 us
    unnamed x12, local copies, waits for them, and re-layouts  2.54 us
    transpose x1, local copies, waits for them, and re-layouts, body(): maps = coil_maps[0].reshape(4, 4, 2, 128, 2, 64).transpose(5, 4, 1, 0, 2, 3)  2.11 us

profile of v5, /device:TPU:1, one launch (start us, length us, event | category | flops | bytes accessed | tf_op | source)
XLA Modules:
  0.0 104.3 jit_solution(1986450246035496090)
XLA Ops:
  0.6 1.5 %copy.17 = bf16[1,16,256,128]{2,3,1,0:T(8,128)(2,1)S(1)} copy(bf16[1,16,256,128]{3,2,1,0:T(8,128)(2,1)} %param.16) | data formatting | bytes 2097152 | tf_op args[2]
  2.1 0.0 copy-start
  2.1 1.6 %copy.29 = bf16[16,256,2,64]{1,0,2,3:T(8,128)(2,1)} copy(bf16[16,256,2,64]{1,3,2,0:T(8,128)(2,1)S(1)} %bitcast.24) | data formatting | bytes 2097152 | tf_op jit(solution)/shard_map/reshape;squeeze | solution.py:673
  3.7 0.0 copy-done
  3.7 0.7 copy.19
  4.4 0.0 copy-start.2
  4.4 0.0 copy-start.1
  4.4 2.1 %copy.20 = bf16[64,2,4,4,2,128]{5,4,3,2,1,0:T(2,128)(2,1)} copy(bf16[64,2,4,4,2,128]{5,0,1,4,2,3:T(8,128)(2,1)S(1)} %bitcast.25) | data formatting | bytes 2097152 | tf_op jit(solution)/shard_map/transpose | solution.py:674
  6.5 0.0 copy-done.2
  6.6 0.1 concatenate.9
  6.7 0.6 pad.47
  7.4 0.0 copy-done.1
  7.4 0.2 copy.22
  7.5 0.2 reshape.34
  7.7 0.1 pad.58.clone
  7.8 0.2 fusion.6
  8.0 0.1 slice.17
  8.0 0.2 copy.27
  8.2 0.0 copy-start.3
  8.2 0.1 slice.16
  8.3 0.2 copy.26
  8.5 0.1 pad.54.clone
  8.6 0.9 maximum_maximum_fusion.w2_ref
  9.5 0.0 copy-done.3
  9.5 0.1 reshape.38
  9.6 0.6 pad_bitcast_fusion.w3_ref
  10.2 92.6 %shard_map.149 = f32[2,128,128]{2,1,0:T(8,128)} custom-call(f32[128,128]{1,0:T(8,128)} %bitcast.32, bf16[64,2,16,256]{3,2,1,0:T(8,128)(2,1)} %bitcast.22, bf16[64,2,4,8,128]{4,3,2,1,0:T(8,128)(2,1)} %bitcast.23, s32[16,256]{1,0:T(8,128)} %sampling_ref.1, bf16[144,256]{1,0:T(8,128)(2,1)} %bitcast.30, bf16[512,384]{1,0:T(8,128)(2,1)} %maximum_maximum_fusion.w2_ref, ...), custom_call_target="tpu_custom_call" | custom-call | tf_op jit(solution)/shard_map/pallas_call | solution.py:702
  102.8 1.5 %fusion.8 = (f32[1,128,128]{2,1,0:T(8,128)}, f32[1,128,128]{2,1,0:T(8,128)}) fusion(f32[2,128,128]{2,1,0:T(8,128)} %shard_map.149), kind=kLoop, calls=%fused_computation.16 | loop fusion | bytes 262144 | tf_op jit(solution)/shard_map/slice | solution.py:774
  (5 shorter events, 0.1 us)
Async XLA Ops:
  2.1 1.6 %copy-start = (bf16[1,32,128,128]{3,2,1,0:T(8,128)(2,1)S(1)}, bf16[1,32,128,128]{3,2,1,0:T(8,128)(2,1)}, u32[]{:S(2)}) copy-start(bf16[1,32,128,128]{3,2,1,0:T(8,128)(2,1)} %param.15) | copy-start | bytes 3145732
  4.4 2.1 %copy-start.2 = (bf16[3,3,3,32,2]{3,4,2,1,0:T(2,128)(2,1)S(1)}, bf16[3,3,3,32,2]{3,4,2,1,0:T(2,128)(2,1)}, u32[]{:S(2)}) copy-start(bf16[3,3,3,32,2]{3,4,2,1,0:T(2,128)(2,1)} %param.18) | copy-start | bytes 10372
  4.4 3.0 %copy-start.1 = (bf16[3,3,3,32,32]{4,3,2,1,0:T(8,128)(2,1)S(1)}, bf16[3,3,3,32,32]{4,3,2,1,0:T(8,128)(2,1)}, u32[]{:S(2)}) copy-start(bf16[3,3,3,32,32]{4,3,2,1,0:T(8,128)(2,1)} %param.20) | copy-start | bytes 165892
  8.2 1.2 %copy-start.3 = (bf16[3,3,3,2,32]{4,3,2,1,0:T(2,128)(2,1)S(1)}, bf16[3,3,3,2,32]{4,3,2,1,0:T(2,128)(2,1)}, u32[]{:S(2)}) copy-start(bf16[3,3,3,2,32]{4,3,2,1,0:T(2,128)(2,1)} %param.22) | copy-start | bytes 10372

commit v6 on v5

--- a/solution.py
+++ b/solution.py
@@ -120,17 +120,27 @@
     k_hbm,
     m_hbm,
     sampling_ref,
-    w1_ref,
-    w2_ref,
-    w3_ref,
+    first_ref,
+    middle_ref,
+    last_ref,
     b1_ref,
     b2_ref,
     b3_ref,
+    fy_hbm,
+    gy_hbm,
+    fz_hbm,
+    gz_hbm,
+    out_ref,
     fy_ref,
     gy_ref,
     fz_ref,
     gz_ref,
-    out_ref,
+    w1_wide,
+    w1_ref,
+    w2_turned,
+    w2_ref,
+    w3_wide,
+    w3_ref,
     k_ref,
     m_ref,
     s_ref,
@@ -227,6 +237,30 @@
                 device_id={"g": lax.rem(g + i, 4), "b": lax.rem(b + c, 2)},
                 device_id_type=mesh_id,
             )
+    table_copies = []
+    for n, (source, target) in enumerate(
+        ((fy_hbm, fy_ref), (gy_hbm, gy_ref), (fz_hbm, fz_ref), (gz_hbm, gz_ref))
+    ):
+        table_copies.append(pltpu.make_async_copy(source, target, local_sem.at[2 + n]))
+        table_copies[n].start()
+    w1_wide[...] = jnp.zeros_like(w1_wide)
+    w2_turned[...] = jnp.zeros_like(w2_turned)
+    w3_wide[...] = jnp.zeros_like(w3_wide)
+    for a in range(3):
+        for tap in range(9):
+            dz, dx = tap // 3, tap % 3
+            value = first_ref[9 * a + tap].astype(f32)
+            for r in range(7):
+                place = 16 * tap + 2 * (min(r, 4) + a)
+                w1_wide[place : place + 2, 32 * r : 32 * r + 32] = value
+            w3_wide[8 * tap : 8 * tap + 2, 32 * a : 32 * a + 32] = last_ref[9 * a + tap].astype(f32)
+            value = middle_ref[9 * a + tap]
+            for r in range(3):
+                place = 128 * dz + 32 * (r + a) if r + a < 4 else 384 + 32 * dz
+                w2_turned[128 * dx + 32 * r : 128 * dx + 32 * r + 32, place : place + 32] = value
+    w1_ref[...] = w1_wide[...].astype(bf16)
+    w2_ref[...] = jnp.transpose(w2_turned[...].astype(f32)).astype(bf16)
+    w3_ref[...] = w3_wide[...].astype(bf16)
     mask_own[...] = sampling_ref[...].astype(f32).astype(bf16)
     left = lanes((64, 128)) < 64
     top, bottom = prior_ref[0:64], prior_ref[64:128]
@@ -379,6 +413,8 @@
     dbuf[pl.ds(me, 1)] = dsrc[pl.ds(me, 1)]
 
     k_local.wait()
+    for copy in table_copies:
+        copy.wait()
     for copy in mask_copies:
         copy.wait()
     order = lax.broadcasted_iota(jnp.int32, (256, 256), 0)
@@ -674,22 +710,6 @@
     maps = coil_maps[0].reshape(4, 4, 2, 128, 2, 64).transpose(5, 4, 1, 0, 2, 3)
     maps = maps.reshape(64, 2, 4, 8, 128)
 
-    first = weight_first.transpose(1, 2, 0, 4, 3).reshape(9, 6, 32)
-    pieces = [jnp.pad(first, ((0, 0), (2 * r, 10 - 2 * r), (0, 0))) for r in (0, 1, 2, 3, 4, 4, 4)]
-    w1 = jnp.pad(jnp.concatenate(pieces, axis=2), ((0, 0), (0, 0), (0, 32))).reshape(144, 256)
-    middle = weight_middle.transpose(1, 0, 4, 2, 3).reshape(3, 96, 3, 32)
-    pieces = [jnp.pad(middle, ((0, 0), (32 * r, 64 - 32 * r), (0, 0), (0, 0))) for r in range(3)]
-    middle = jnp.concatenate(pieces + [jnp.zeros_like(pieces[0])], axis=3).reshape(3, 160, 384)
-    w2 = jnp.concatenate(
-        [
-            middle[:, :128].reshape(384, 384),
-            middle[:, 128:].reshape(96, 384),
-            jnp.zeros((32, 384), bf16),
-        ],
-        axis=0,
-    )
-    w3 = weight_last.transpose(1, 2, 3, 0, 4).reshape(9, 2, 96)
-    w3 = jnp.pad(w3, ((0, 0), (0, 6), (0, 32))).reshape(72, 128)
     b1 = bias_first[None]
     b2 = bias_middle[None]
 
@@ -702,9 +722,19 @@
     out = pl.pallas_call(
         step_kernel,
         out_shape=out,
-        in_specs=[vmem] + [hbm] * 2 + [vmem] * 6 + [smem] + [vmem] * 4,
+        in_specs=[vmem] + [hbm] * 2 + [vmem] * 6 + [smem] + [hbm] * 4,
         out_specs=vmem,
         scratch_shapes=[
+            pltpu.VMEM((2, 2, 256, 256), bf16),
+            pltpu.VMEM((2, 2, 256, 256), bf16),
+            pltpu.VMEM((2, 256, 256), bf16),
+            pltpu.VMEM((2, 256, 256), bf16),
+            pltpu.VMEM((144, 256), f32),
+            pltpu.VMEM((144, 256), bf16),
+            pltpu.VMEM((384, 512), bf16),
+            pltpu.VMEM((512, 384), bf16),
+            pltpu.VMEM((72, 128), f32),
+            pltpu.VMEM((72, 128), bf16),
             pltpu.VMEM((64, 2, 16, 256), bf16),
             pltpu.VMEM((64, 2, 4, 8, 128), bf16),
             pltpu.VMEM((8, 2, 256, 128), f32),
@@ -750,7 +780,7 @@
             dma((6,)),
             dma((4,)),
             dma((4,)),
-            dma((2,)),
+            dma((6,)),
         ],
         compiler_params=pltpu.CompilerParams(
             collective_id=0, has_side_effects=True, vmem_limit_bytes=60 * 1024 * 1024
@@ -760,9 +790,9 @@
         spectrum,
         maps,
         sampling,
-        w1,
-        w2,
-        w3,
+        weight_first.transpose(0, 1, 2, 4, 3).reshape(27, 2, 32),
+        weight_middle.reshape(27, 32, 32),
+        weight_last.reshape(27, 2, 32),
         b1,
         b2,
         bias_last,

time: 105 us -> 100 us (0.952)
  local copies, waits for them, and re-layouts: 9.89 us -> 7.34 us
  other arithmetic: 1.06 us -> 0 us
    concatenate x2 -> x0, other arithmetic: 1.06 us -> none  [the longest x1 0.88 us: body(): jnp.concatenate([middle[:, :128].reshape(384, 384), middle[:, 128:].resha...]
    unnamed x12 -> x4, local copies, waits for them, and re-layouts: 2.54 us -> 2.15 us
where the time goes in v6:
time: 100 us; the launch traced here: 99.8 us
  Pallas kernels  91.8 us (92%)
  local copies, waits for them, and re-layouts  7.34 us (7%)
    pallas_call x1, Pallas kernels, body(): pl.pallas_call(step_kernel, out_shape=out, in_specs=[vmem] + [hbm] * 2 +...  91.8 us
    unnamed x4, local copies, waits for them, and re-layouts  2.15 us
    transpose x1, local copies, waits for them, and re-layouts, body(): maps = coil_maps[0].reshape(4, 4, 2, 128, 2, 64).transpose(5, 4, 1, 0, 2, 3)  2.11 us

profile of v6, /device:TPU:1, one launch (start us, length us, event | category | flops | bytes accessed | tf_op | source)
XLA Modules:
  0.0 99.8 jit_solution(9968788513118807489)
XLA Ops:
  0.6 1.6 %copy.19 = bf16[1,32,128,128]{2,3,1,0:T(8,128)(2,1)S(1)} copy(bf16[1,32,128,128]{3,2,1,0:T(8,128)(2,1)} %param.15) | data formatting | bytes 2097152 | tf_op args[1]
  2.3 0.0 copy-start
  2.3 2.1 %copy.20 = bf16[64,2,4,4,2,128]{5,4,3,2,1,0:T(2,128)(2,1)} copy(bf16[64,2,4,4,2,128]{5,0,1,4,2,3:T(8,128)(2,1)S(1)} %bitcast.18) | data formatting | bytes 2097152 | tf_op jit(solution)/shard_map/transpose | solution.py:710
  4.4 0.0 copy-done
  4.4 0.5 copy.17
  4.9 1.6 %copy.22 = bf16[16,256,2,64]{1,0,2,3:T(8,128)(2,1)} copy(bf16[16,256,2,64]{1,3,2,0:T(8,128)(2,1)S(1)} %bitcast.19) | data formatting | bytes 2097152 | tf_op jit(solution)/shard_map/reshape;squeeze | solution.py:709
  6.5 91.8 %shard_map.149 = f32[2,128,128]{2,1,0:T(8,128)} custom-call(f32[128,128]{1,0:T(8,128)} %bitcast.21, bf16[64,2,16,256]{3,2,1,0:T(8,128)(2,1)} %bitcast.17, bf16[64,2,4,8,128]{4,3,2,1,0:T(8,128)(2,1)} %bitcast.16, s32[16,256]{1,0:T(8,128)} %sampling_ref.1, bf16[27,2,32]{2,1,0:T(2,128)(2,1)} %bitcast.22, bf16[27,32,32]{2,1,0:T(8,128)(2,1)} %bitcast.20, ...), custom_call_target="tpu_custom_call" | custom-call | tf_op jit(solution)/shard_map/pallas_call | solution.py:722
  98.3 1.5 %fusion = (f32[1,128,128]{2,1,0:T(8,128)}, f32[1,128,128]{2,1,0:T(8,128)}) fusion(f32[2,128,128]{2,1,0:T(8,128)} %shard_map.149), kind=kLoop, calls=%fused_computation.1 | loop fusion | bytes 262144 | tf_op jit(solution)/shard_map/slice | solution.py:804
Async XLA Ops:
  2.3 2.1 %copy-start = (bf16[1,16,256,128]{3,2,1,0:T(8,128)(2,1)S(1)}, bf16[1,16,256,128]{3,2,1,0:T(8,128)(2,1)}, u32[]{:S(2)}) copy-start(bf16[1,16,256,128]{3,2,1,0:T(8,128)(2,1)} %param.16) | copy-start | bytes 3145732

commit v7 on v6

--- a/solution.py
+++ b/solution.py
@@ -359,7 +359,7 @@
             )
         return 0
 
-    lax.fori_loop(0, 16, layer_one, 0)
+    lax.fori_loop(0, 16, layer_one, 0, unroll=2)
     zero = jnp.zeros((64, 128), bf16)
     h1m[0:64] = zero
     h1m[64:128] = h1m[128 + 8064 : 128 + 8128]
@@ -660,10 +660,10 @@
         forward_rows(g, direction)
         for i in (1, 3, 2):
             forward_rows(*finish(i))
-        energy = lax.fori_loop(0, 4, forward_pair, jnp.zeros((8, 128), f32), unroll=2)
+        energy = lax.fori_loop(0, 4, forward_pair, jnp.zeros((8, 128), f32), unroll=4)
         stats = [jnp.sum(value, axis=0, keepdims=True) for value in (norm, energy)]
         finish_plane = plane_total(step, jnp.concatenate(stats, axis=0))
-        lax.fori_loop(0, 4, inverse_pair, 0, unroll=2)
+        lax.fori_loop(0, 4, inverse_pair, 0, unroll=4)
         last = []
         image = reduce_scatter(
             step + 1, lambda: last.append(line_total(step, finish_plane()))

time: 100 us -> 100 us (level)
  no operation moved by 1% of the time
where the time goes in v7:
time: 100 us
  Pallas kernels  92 us (92%)
  local copies, waits for them, and re-layouts  7.34 us (7%)
    pallas_call x1, Pallas kernels, body(): pl.pallas_call(step_kernel, out_shape=out, in_specs=[vmem] + [hbm] * 2 +...  92 us
    unnamed x4, local copies, waits for them, and re-layouts  2.15 us
    transpose x1, local copies, waits for them, and re-layouts, body(): maps = coil_maps[0].reshape(4, 4, 2, 128, 2, 64).transpose(5, 4, 1, 0, 2, 3)  2.11 us

profile of v7, /device:TPU:1, one launch (start us, length us, event | category | flops | bytes accessed | tf_op | source)
XLA Modules:
  0.0 100.0 jit_solution(6713520835435099554)
XLA Ops:
  0.6 1.6 %copy.19 = bf16[1,32,128,128]{2,3,1,0:T(8,128)(2,1)S(1)} copy(bf16[1,32,128,128]{3,2,1,0:T(8,128)(2,1)} %param.15) | data formatting | bytes 2097152 | tf_op args[1]
  2.3 0.0 copy-start
  2.3 2.1 %copy.20 = bf16[64,2,4,4,2,128]{5,4,3,2,1,0:T(2,128)(2,1)} copy(bf16[64,2,4,4,2,128]{5,0,1,4,2,3:T(8,128)(2,1)S(1)} %bitcast.18) | data formatting | bytes 2097152 | tf_op jit(solution)/shard_map/transpose | solution.py:710
  4.4 0.0 copy-done
  4.4 0.5 copy.17
  4.9 1.6 %copy.22 = bf16[16,256,2,64]{1,0,2,3:T(8,128)(2,1)} copy(bf16[16,256,2,64]{1,3,2,0:T(8,128)(2,1)S(1)} %bitcast.19) | data formatting | bytes 2097152 | tf_op jit(solution)/shard_map/reshape;squeeze | solution.py:709
  6.5 92.0 %shard_map.149 = f32[2,128,128]{2,1,0:T(8,128)} custom-call(f32[128,128]{1,0:T(8,128)} %bitcast.21, bf16[64,2,16,256]{3,2,1,0:T(8,128)(2,1)} %bitcast.17, bf16[64,2,4,8,128]{4,3,2,1,0:T(8,128)(2,1)} %bitcast.16, s32[16,256]{1,0:T(8,128)} %sampling_ref.1, bf16[27,2,32]{2,1,0:T(2,128)(2,1)} %bitcast.22, bf16[27,32,32]{2,1,0:T(8,128)(2,1)} %bitcast.20, ...), custom_call_target="tpu_custom_call" | custom-call | tf_op jit(solution)/shard_map/pallas_call | solution.py:722
  98.5 1.5 %fusion = (f32[1,128,128]{2,1,0:T(8,128)}, f32[1,128,128]{2,1,0:T(8,128)}) fusion(f32[2,128,128]{2,1,0:T(8,128)} %shard_map.149), kind=kLoop, calls=%fused_computation.1 | loop fusion | bytes 262144 | tf_op jit(solution)/shard_map/slice | solution.py:804
Async XLA Ops:
  2.3 2.1 %copy-start = (bf16[1,16,256,128]{3,2,1,0:T(8,128)(2,1)S(1)}, bf16[1,16,256,128]{3,2,1,0:T(8,128)(2,1)}, u32[]{:S(2)}) copy-start(bf16[1,16,256,128]{3,2,1,0:T(8,128)(2,1)} %param.16) | copy-start | bytes 3145732
